TPU v7x, 32 devices: a whole 2x2x4 slice. The times are simulated.
32 devices in a mesh: dp: 16 (over z, y, x), tensor: 2 (over core).
Axes of the slice: x: 2, y: 2, z: 4, core: 2. Of those that a mesh axis runs over, the one named last changes fastest.
Arguments:
- block_input: bfloat16 [8192, 768], P('dp'), may hold values from -6 to 6
- sequence_ids: int32 [8192], P('dp'), may hold values from 0 to 1, as said below
- attention_gain: float32 [768], replicated, may hold values from 0.25 to 1.75
- attention_shift: float32 [768], replicated, may hold values from -2 to 2
- packed_weight: bfloat16 [768, 3, 768], P(None, None, 'tensor'), may hold values from -0.21875 to 0.21875
- packed_bias: float32 [3, 768], P(None, 'tensor'), may hold values from -3 to 3
- output_weight: bfloat16 [768, 768], P('tensor'), may hold values from -1.75 to 1.75
- output_bias: float32 [768], replicated, may hold values from -3 to 3
- feedforward_gain: float32 [768], replicated, may hold values from 0.25 to 1.75
- feedforward_shift: float32 [768], replicated, may hold values from -2 to 2
- expand_weight: bfloat16 [768, 3072], P(None, 'tensor'), may hold values from -0.21875 to 0.21875
- expand_bias: float32 [3072], P('tensor'), may hold values from -3 to 3
- shrink_weight: bfloat16 [3072, 768], P('tensor'), may hold values from -0.109375 to 0.109375
- shrink_bias: float32 [768], replicated, may hold values from -3 to 3
- grad_output: bfloat16 [8192, 768], P('dp'), may hold values from -6 to 6
Outputs:
- block_output: bfloat16 [8192, 768], P('dp')
- grad_input: bfloat16 [8192, 768], P('dp')
- grad_attention_gain: float32 [768], replicated
- grad_attention_shift: float32 [768], replicated
- grad_packed_weight: float32 [768, 3, 768], P(None, None, 'tensor')
- grad_packed_bias: float32 [3, 768], P(None, 'tensor')
- grad_output_weight: float32 [768, 768], P('tensor')
- grad_output_bias: float32 [768], replicated
- grad_feedforward_gain: float32 [768], replicated
- grad_feedforward_shift: float32 [768], replicated
- grad_expand_weight: float32 [768, 3072], P(None, 'tensor')
- grad_expand_bias: float32 [3072], P('tensor')
- grad_shrink_weight: float32 [3072, 768], P('tensor')
- grad_shrink_bias: float32 [768], replicated
Inputs may be any that keep to these rules, and one draw needn't show every extreme that they name: `sequence_ids`: in each block of 512 rows along the tokens (the rows of one index of dp), tokens with equal values form one sequence in order: the value is 0 on the first 256 rows, and on the other 256 rows either 0 throughout (one sequence of 512) or 1 throughout (two sequences of 256); the first block is always of the second kind.
All inputs are finite; a program needn't handle non-finite values.
Results may differ from a plain program's by a relative error of at most 0.013.
The roundings to bfloat16 on the way count: a program that leaves them out, or rounds other values in their place, can miss the bound.
Values sent between devices are 32-bit elements; how exact they have to be, the bound alone decides.
A program may use at most 128 MiB of HBM per device.

v0:
```python
import math

import jax
import jax.numpy as jnp
from jax import lax
from jax.sharding import PartitionSpec as P

HEAD = 64


EPSILON = 1e-05
MASKED = -1000000000.0


def norm_rows(values_in):
    row_mean = jnp.mean(values_in, axis=-1, keepdims=True)
    centred = values_in - row_mean
    inv_std = lax.rsqrt(jnp.mean(centred * centred, axis=-1, keepdims=True) + EPSILON)
    return (centred * inv_std, inv_std)


def norm_back(grad_normed, normed, inv_std, gain_vector):
    scaled = grad_normed * gain_vector
    centred = scaled - jnp.mean(scaled, axis=-1, keepdims=True)
    return (centred - normed * jnp.mean(scaled * normed, axis=-1, keepdims=True)) * inv_std


def rotary_tables(block_ids, head_size):
    earlier = (block_ids[None, :] < block_ids[:, None]).astype(jnp.int32)
    places = jnp.arange(block_ids.shape[0], dtype=jnp.int32) - jnp.sum(earlier, axis=1)
    half_size = head_size // 2
    frequency = jnp.exp(
        jnp.arange(half_size, dtype=jnp.float32) * (-2.0 * math.log(10000.0) / head_size)
    )
    angles = places.astype(jnp.float32)[:, None] * frequency[None, :]
    return (jnp.cos(angles), jnp.sin(angles))


def rotate(heads_in, cosine, sine_part):
    half_size = heads_in.shape[-1] // 2
    front_half = heads_in[..., :half_size]
    back_half = heads_in[..., half_size:]
    cos_rows = cosine[:, None, :]
    sin_rows = sine_part[:, None, :]
    return jnp.concatenate(
        [
            front_half * cos_rows - back_half * sin_rows,
            back_half * cos_rows + front_half * sin_rows,
        ],
        axis=-1,
    )


def rotate_back(grads_in, cosine, sine_part):
    half_size = grads_in.shape[-1] // 2
    front_half = grads_in[..., :half_size]
    back_half = grads_in[..., half_size:]
    cos_rows = cosine[:, None, :]
    sin_rows = sine_part[:, None, :]
    return jnp.concatenate(
        [
            front_half * cos_rows + back_half * sin_rows,
            back_half * cos_rows - front_half * sin_rows,
        ],
        axis=-1,
    )


def body(
    block_input,
    sequence_ids,
    attention_gain,
    attention_shift,
    packed_weight,
    packed_bias,
    output_weight,
    output_bias,
    feedforward_gain,
    feedforward_shift,
    expand_weight,
    expand_bias,
    shrink_weight,
    shrink_bias,
    grad_output,
):
    token_count = block_input.shape[0]
    local_width = packed_weight.shape[2]
    local_heads = local_width // HEAD
    score_scale = HEAD ** (-0.5)
    contract_rows = (((0,), (0,)), ((), ()))
    contract_cols = (((1,), (1,)), ((), ()))
    residual = block_input.astype(jnp.float32)
    normed_a, inv_std_a = norm_rows(residual)
    attend_in = (normed_a * attention_gain + attention_shift).astype(jnp.bfloat16)
    cosine, sine_part = rotary_tables(sequence_ids, HEAD)
    same_sequence = (sequence_ids[:, None] == sequence_ids[None, :])[None]
    packed = (
        jnp.einsum("td,dcw->tcw", attend_in, packed_weight, preferred_element_type=jnp.float32)
        + packed_bias
    )
    split_heads = packed.reshape(token_count, 3, local_heads, HEAD)
    queries = rotate(split_heads[:, 0], cosine, sine_part).astype(jnp.bfloat16)
    keys_rot = rotate(split_heads[:, 1], cosine, sine_part).astype(jnp.bfloat16)
    values_low = split_heads[:, 2].astype(jnp.bfloat16)
    scores = (
        jnp.einsum("qhd,khd->hqk", queries, keys_rot, preferred_element_type=jnp.float32)
        * score_scale
    )
    scores = jnp.where(same_sequence, scores, MASKED)
    row_max = jnp.max(scores, axis=-1, keepdims=True)
    log_total = row_max + jnp.log(jnp.sum(jnp.exp(scores - row_max), axis=-1, keepdims=True))
    prob_full = jnp.exp(scores - log_total)
    prob_low = prob_full.astype(jnp.bfloat16)
    attended = jnp.einsum("hqk,khd->qhd", prob_low, values_low, preferred_element_type=jnp.float32)
    attended = attended.reshape(token_count, local_width).astype(jnp.bfloat16)
    mixed = lax.psum(jnp.dot(attended, output_weight, preferred_element_type=jnp.float32), "tensor")
    middle = residual + mixed + output_bias
    normed_b, inv_std_b = norm_rows(middle)
    expand_in = (normed_b * feedforward_gain + feedforward_shift).astype(jnp.bfloat16)
    pre_act = jnp.dot(expand_in, expand_weight, preferred_element_type=jnp.float32) + expand_bias
    activated, gelu_pull = jax.vjp(lambda inner: jax.nn.gelu(inner, approximate=False), pre_act)
    act_low = activated.astype(jnp.bfloat16)
    shrunk = lax.psum(jnp.dot(act_low, shrink_weight, preferred_element_type=jnp.float32), "tensor")
    block_output = (middle + shrunk + shrink_bias).astype(jnp.bfloat16)
    top_grad = grad_output.astype(jnp.float32)
    grad_shrink_bias = jnp.sum(top_grad, axis=0)
    grad_shrink_weight = lax.dot_general(
        act_low, grad_output, contract_rows, preferred_element_type=jnp.float32
    )
    grad_act = lax.dot_general(
        grad_output, shrink_weight, contract_cols, preferred_element_type=jnp.float32
    )
    grad_pre = gelu_pull(grad_act)[0].astype(jnp.bfloat16)
    grad_expand_bias = jnp.sum(grad_pre.astype(jnp.float32), axis=0)
    grad_expand_weight = lax.dot_general(
        expand_in, grad_pre, contract_rows, preferred_element_type=jnp.float32
    )
    grad_expand_in = lax.psum(
        lax.dot_general(grad_pre, expand_weight, contract_cols, preferred_element_type=jnp.float32),
        "tensor",
    )
    grad_feedforward_gain = jnp.sum(grad_expand_in * normed_b, axis=0)
    grad_feedforward_shift = jnp.sum(grad_expand_in, axis=0)
    grad_middle = top_grad + norm_back(grad_expand_in, normed_b, inv_std_b, feedforward_gain)
    grad_output_bias = jnp.sum(grad_middle, axis=0)
    grad_mixed = grad_middle.astype(jnp.bfloat16)
    grad_output_weight = lax.dot_general(
        attended, grad_mixed, contract_rows, preferred_element_type=jnp.float32
    )
    grad_attended = lax.dot_general(
        grad_mixed, output_weight, contract_cols, preferred_element_type=jnp.float32
    )
    grad_attended = grad_attended.astype(jnp.bfloat16).reshape(token_count, local_heads, HEAD)
    grad_probs = jnp.einsum(
        "qhd,khd->hqk", grad_attended, values_low, preferred_element_type=jnp.float32
    )
    row_inner = jnp.sum(prob_full * grad_probs, axis=-1, keepdims=True)
    grad_scores = (prob_full * (grad_probs - row_inner)).astype(jnp.bfloat16)
    grad_values = jnp.einsum(
        "hqk,qhd->khd", prob_low, grad_attended, preferred_element_type=jnp.float32
    )
    grad_queries = (
        jnp.einsum("hqk,khd->qhd", grad_scores, keys_rot, preferred_element_type=jnp.float32)
        * score_scale
    )
    grad_keys = (
        jnp.einsum("hqk,qhd->khd", grad_scores, queries, preferred_element_type=jnp.float32)
        * score_scale
    )
    grad_packed = jnp.stack(
        [
            rotate_back(grad_queries, cosine, sine_part),
            rotate_back(grad_keys, cosine, sine_part),
            grad_values,
        ],
        axis=1,
    )
    grad_packed = grad_packed.reshape(token_count, 3, local_width).astype(jnp.bfloat16)
    grad_packed_bias = jnp.sum(grad_packed.astype(jnp.float32), axis=0)
    grad_packed_weight = jnp.einsum(
        "td,tcw->dcw", attend_in, grad_packed, preferred_element_type=jnp.float32
    )
    grad_attend_in = lax.psum(
        jnp.einsum("tcw,dcw->td", grad_packed, packed_weight, preferred_element_type=jnp.float32),
        "tensor",
    )
    grad_attention_gain = jnp.sum(grad_attend_in * normed_a, axis=0)
    grad_attention_shift = jnp.sum(grad_attend_in, axis=0)
    grad_input = (
        grad_middle + norm_back(grad_attend_in, normed_a, inv_std_a, attention_gain)
    ).astype(jnp.bfloat16)
    every_grad = lax.psum(
        (
            grad_attention_gain,
            grad_attention_shift,
            grad_packed_weight,
            grad_packed_bias,
            grad_output_weight,
            grad_output_bias,
            grad_feedforward_gain,
            grad_feedforward_shift,
            grad_expand_weight,
            grad_expand_bias,
            grad_shrink_weight,
            grad_shrink_bias,
        ),
        "dp",
    )
    return (
        block_output,
        grad_input,
        every_grad[0],
        every_grad[1],
        every_grad[2],
        every_grad[3],
        every_grad[4],
        every_grad[5],
        every_grad[6],
        every_grad[7],
        every_grad[8],
        every_grad[9],
        every_grad[10],
        every_grad[11],
    )


def solution(mesh):
    in_specs = (
        P("dp", None),
        P("dp"),
        P(),
        P(),
        P(None, None, "tensor"),
        P(None, "tensor"),
        P("tensor", None),
        P(),
        P(),
        P(),
        P(None, "tensor"),
        P("tensor"),
        P("tensor", None),
        P(),
        P("dp", None),
    )
    out_specs = (
        P("dp", None),
        P("dp", None),
        P(),
        P(),
        P(None, None, "tensor"),
        P(None, "tensor"),
        P("tensor", None),
        P(),
        P(),
        P(),
        P(None, "tensor"),
        P("tensor"),
        P("tensor", None),
        P(),
    )
    return jax.shard_map(body, mesh=mesh, in_specs=in_specs, out_specs=out_specs, check_vma=False)
```

profile of v0, /device:TPU:0, one launch (start us, length us, event | category | flops | bytes accessed | tf_op | source)
XLA Modules:
  0.0 569.4 jit_solution(17436027513775236693)
XLA Ops:
  7.3 1.1 broadcast_compare_fusion
  8.3 0.9 convert_reduce_fusion.4
  9.3 1.3 convert_reduce_fusion.1
  10.6 1.5 fusion.22
  12.1 3.0 convolution_add_fusion.1
  15.3 0.3 multiply_cosine_fusion
  15.6 0.3 subtract_convert_fusion.3
  15.9 0.6 copy-done.33
  16.6 1.2 fusion
  17.8 1.3 exponential_reduce_fusion
  19.2 1.3 copy-done.2
  20.5 1.7 convolution_convert_fusion.2
  22.2 0.7 copy-done.18
  23.0 1.7 fusion.48
  24.8 23.2 %all-reduce.8.cloned.1.call-done = f32[512,768]{1,0:T(8,128)} async-done(((f32[512,768]{1,0:T(8,128)}), f32[512,768]{1,0:T(8,128)}) %all-reduce.8.cloned.1.call-update) | async-done | bytes 1572880 | tf_op jit(solution)/shard_map/psum | solution.py:116
  48.0 1.8 fusion.46
  49.8 0.3 multiply_reduce_fusion.3
  50.2 0.9 copy-done.3
  51.1 1.5 convolution_add_fusion
  52.6 10.1 %convert_reduce_fusion = (f32[1536]{0:T(1024)}, bf16[512,1536]{1,0:T(8,128)(2,1)S(1)}, f32[512,1536]{1,0:T(8,128)}) fusion(f32[512,1536]{1,0:T(8,128)S(1)} %convolution_add_fusion, bf16[512,768]{1,0:T(8,128)(2,1)S(1)} %copy-done.13, bf16[1536,768]{1,0:T(8,128)(2,1)S(1)} %copy-done), kind=kOutput, calls=%fused_computation.10 | convolution fusion | flops 1266153984 | bytes 11016192 | tf_op jit(solution)/shard_map/dot_general | solution.py:130
  62.8 1.1 copy-done.51
  63.9 2.6 fusion.50
  66.5 0.2 all-reduce.14.cloned.1.call-start
  66.8 3.6 multiply_convert_fusion.1
  70.3 1.1 copy-done.8
  71.5 2.5 fusion.49
  74.0 14.2 %all-reduce.10.cloned.1.call-done = f32[512,768]{1,0:T(8,128)} async-done(((f32[512,768]{1,0:T(8,128)}), f32[512,768]{1,0:T(8,128)}) %all-reduce.10.cloned.1.call-update) | async-done | bytes 1572880 | tf_op jit(solution)/shard_map/psum | solution.py:138
  88.2 3.3 multiply_reduce_fusion.1
  91.5 2.5 fusion.45
  94.1 1.2 copy-done.5
  95.3 0.5 convolution_convert_fusion.1
  95.8 5.5 convolution_convert_fusion
  101.3 5.8 %multiply_reduce_fusion = (f32[6,512]{1,0:T(8,128)S(1)}, f32[6,512,512]{1,2,0:T(8,128)}) fusion(f32[6,512,512]{1,2,0:T(8,128)S(1)} %bitcast.52, f32[6,512]{1,0:T(8,128)S(1)} %log_add_fusion, pred[512,512]{0,1:T(8,128)(4,1)S(1)} %broadcast_compare_fusion, bf16[512,6,64]{0,2,1:T(8,128)(2,1)S(1)} %bitcast.59, f32[512,3,6,64]{0,3,2,1:T(8,128)} %bitcast.57), kind=kOutput, calls=%fused_computation.1 | convolution fusion | flops 209187840 | bytes 13656064 | tf_op jit(solution)/shard_map/qhd,khd->hqk/dot_general | solution.py:154
  107.0 4.7 multiply_convert_fusion
  111.8 0.6 fusion.25
  112.4 0.3 copy-done.26
  112.8 1.9 fusion.24
  114.8 1.2 copy.36
  116.0 2.2 add_convert_fusion.4
  118.2 0.2 copy.35
  118.4 1.2 pad_maximum_fusion.3
  119.6 0.9 copy.34
  120.6 4.0 convolution_bitcast_fusion
  124.6 0.3 all-reduce.12.cloned.1.call-start
  124.8 0.8 copy-done.14
  125.7 5.1 fusion.51
  130.9 3.8 fusion.43
  134.7 1.5 fusion.28
  136.2 3.2 fusion.32
  139.5 1.0 copy-done.23
  140.4 0.2 convert_reduce_fusion.2
  140.7 8.6 %all-reduce.14.cloned.1.call-done = (f32[512,768]{1,0:T(8,128)}, f32[512,768]{1,0:T(8,128)}) async-done(((f32[512,768]{1,0:T(8,128)}, f32[512,768]{1,0:T(8,128)}), (f32[512,768]{1,0:T(8,128)}, f32[512,768]{1,0:T(8,128)})) %all-reduce.14.cloned.1.call-update) | async-done | bytes 3145744 | tf_op jit(solution)/shard_map/psum | solution.py:123
  149.3 2.2 fusion.21
  151.5 81.9 %all-reduce = (f32[768]{0:T(1024)}, f32[768]{0:T(1024)}, f32[3,384]{1,0:T(4,128)}, f32[768]{0:T(1024)}, f32[768]{0:T(1024)}, /*index=5*/f32[768]{0:T(1024)}, f32[1536]{0:T(1024)}, f32[768]{0:T(1024)}) all-reduce(f32[768]{0:T(1024)S(1)} %get-tuple-element.16, ...), channel_id=1, replica_groups=mesh['dp'=16,'tensor'=2] {'dp'}, use_global_device_ids=true, to_apply=%region_17.18 | all-reduce | flops 7296 | bytes 58368 | tf_op jit(solution)/shard_map/psum | solution.py:192
  233.4 2.6 add_convert_fusion.1
  236.0 3.0 fusion.20
  239.0 311.9 %all-reduce.12.cloned.1.call-done = (f32[768,3,384]{2,0,1:T(8,128)}, f32[384,768]{1,0:T(8,128)}, f32[768,1536]{1,0:T(8,128)}, f32[1536,768]{1,0:T(8,128)}) async-done(((f32[768,3,384]{2,0,1:T(8,128)}, f32[384,768]{1,0:T(8,128)}, f32[768,1536]{1,0:T(8,128)}, f32[1536,768]{1,0:T(8,128)}), (f32[768,3,384]{2,0,1:T(8,128)}, f32[384,768]{1,0:T(8,128)}, f32[768,1536]{1,0:T(8,128)}, ...) | async-done | bytes 14155792 | tf_op jit(solution)/shard_map/psum | solution.py:192
  550.9 4.2 copy.53
  555.1 1.0 copy.54
  556.1 2.4 copy.55
  558.5 0.8 slice-done.2
  559.3 0.2 slice-done.3
  559.5 2.4 copy.56
  561.9 1.0 copy-done.1
  (121 shorter events, 0.7 us)
Async XLA Ops:
  7.2 45.4 %copy-start = (bf16[1536,768]{1,0:T(8,128)(2,1)S(1)}, bf16[1536,768]{1,0:T(8,128)(2,1)}, u32[]{:S(2)}) copy-start(bf16[1536,768]{1,0:T(8,128)(2,1)} %param.27) | copy-start | bytes 7077892
  7.2 40.8 %all-reduce.8.cloned.1.call-start = ((), (), s32[]{:S(2)}) async-start(), calls=%async_computation | async-start | bytes 3145728 | tf_op jit(solution)/shard_map/psum | solution.py:116
  15.1 4.0 copy-start.17
  15.6 0.9 copy-start.33
  15.6 0.9 copy-start.34
  15.9 1.9 copy-start.25
  15.9 1.9 copy-start.27
  15.9 1.9 copy-start.29
  15.9 1.9 copy-start.31
  17.8 2.7 copy-start.2
  20.5 2.5 copy-start.15
  22.2 0.7 copy-start.18
  22.2 25.8 %copy-start.7 = (bf16[512,768]{1,0:T(8,128)(2,1)S(1)}, bf16[512,768]{1,0:T(8,128)(2,1)}, u32[]{:S(2)}) copy-start(bf16[512,768]{1,0:T(8,128)(2,1)} %param.15) | copy-start | bytes 2359300
  22.2 25.7 %copy-start.45 = (f32[768]{0:T(1024)S(1)}, f32[768]{0:T(1024)}, u32[]{:S(2)}) copy-start(f32[768]{0:T(1024)} %param.22) | copy-start | bytes 9220
  24.7 26.3 %copy-start.35 = (f32[768]{0:T(1024)S(1)}, f32[768]{0:T(1024)}, u32[]{:S(2)}) copy-start(f32[768]{0:T(1024)} %param.23) | copy-start | bytes 9220
  24.7 26.3 %copy-start.47 = (f32[1536]{0:T(1024)S(1)}, f32[1536]{0:T(1024)}, u32[]{:S(2)}) copy-start(f32[1536]{0:T(1024)} %param.26) | copy-start | bytes 18436
  24.7 26.3 %copy-start.48 = (f32[768]{0:T(1024)S(1)}, f32[768]{0:T(1024)}, u32[]{:S(2)}) copy-start(f32[768]{0:T(1024)} %param.24) | copy-start | bytes 9220
  24.8 63.5 %all-reduce.10.cloned.1.call-start = ((), (), s32[]{:S(2)}) async-start(), calls=%async_computation.1 | async-start | bytes 3145728 | tf_op jit(solution)/shard_map/psum | solution.py:138
  48.0 3.1 copy-start.46
  49.8 1.2 copy-start.3
  51.1 1.5 copy-start.13
  52.6 10.2 %copy-start.12 = (f32[512,1536]{1,0:T(8,128)}, f32[512,1536]{1,0:T(8,128)S(1)}, u32[]{:S(2)}) copy-start(f32[512,1536]{1,0:T(8,128)S(1)} %convolution_add_fusion) | copy-start | bytes 9437188
  62.8 1.1 copy-start.51
  66.5 82.7 %all-reduce.14.cloned.1.call-start = ((), (), s32[]{:S(2)}) async-start(), calls=%async_computation.3 | async-start | bytes 6291456 | tf_op jit(solution)/shard_map/psum | solution.py:123
  70.3 1.1 copy-start.8
  74.0 17.5 %copy-start.4 = (f32[512,768]{1,0:T(8,128)S(1)}, f32[512,768]{1,0:T(8,128)}, u32[]{:S(2)}) copy-start(f32[512,768]{1,0:T(8,128)} %copy-done.3) | copy-start | bytes 4718596
  88.2 3.3 copy-start.10
  91.5 3.7 copy-start.16
  94.1 1.2 copy-start.5
  95.3 6.0 %slice-start = ((s8[6291456]{0:T(1024)(128)(4,1)}), s8[4194304]{0:T(1024)(128)(4,1)S(1)}, s32[]{:S(2)}) async-start(s8[6291456]{0:T(1024)(128)(4,1)} %bitcast.51), calls=%async_computation.4 | async-start | bytes 8388608
  95.8 5.5 slice-start.1
  107.0 4.8 copy-start.30
  107.0 4.8 copy-start.32
  111.8 0.9 copy-start.26
  111.8 1.0 copy-start.28
  118.4 2.1 copy-start.20
  124.5 1.1 copy-start.14
  124.6 426.3 %all-reduce.12.cloned.1.call-start = ((), (), s32[]{:S(2)}) async-start(), calls=%async_computation.2 | async-start | bytes 28311552 | tf_op jit(solution)/shard_map/psum | solution.py:192
  125.7 5.1 copy-start.36
  125.7 5.1 copy-start.49
  125.7 5.1 copy-start.52
  130.8 3.9 copy-start.6
  130.8 3.8 copy-start.19
  134.7 1.5 copy-start.21
  134.7 1.5 copy-start.22
  134.7 1.5 copy-start.41
  134.7 1.5 copy-start.50
  139.5 1.0 copy-start.23
  140.6 10.8 %copy-start.37 = (f32[768]{0:T(1024)S(1)}, f32[768]{0:T(1024)}, u32[]{:S(2)}) copy-start(f32[768]{0:T(1024)} %get-tuple-element.14) | copy-start | bytes 9220
  140.6 10.8 %copy-start.38 = (f32[768]{0:T(1024)S(1)}, f32[768]{0:T(1024)}, u32[]{:S(2)}) copy-start(f32[768]{0:T(1024)} %get-tuple-element.20) | copy-start | bytes 9220
  140.7 10.8 %copy-start.39 = (f32[768]{0:T(1024)S(1)}, f32[768]{0:T(1024)}, u32[]{:S(2)}) copy-start(f32[768]{0:T(1024)} %get-tuple-element.39) | copy-start | bytes 9220
  140.7 10.8 %copy-start.40 = (f32[768]{0:T(1024)S(1)}, f32[768]{0:T(1024)}, u32[]{:S(2)}) copy-start(f32[768]{0:T(1024)} %get-tuple-element.53) | copy-start | bytes 9220
  140.7 10.8 %copy-start.43 = (f32[1536]{0:T(1024)S(1)}, f32[1536]{0:T(1024)}, u32[]{:S(2)}) copy-start(f32[1536]{0:T(1024)} %get-tuple-element.36) | copy-start | bytes 18436
  140.7 92.7 %copy-start.44 = (f32[768]{0:T(1024)S(1)}, f32[768]{0:T(1024)}, u32[]{:S(2)}) copy-start(f32[768]{0:T(1024)} %param.28) | copy-start | bytes 9220
  151.4 84.6 %copy-start.42 = (f32[768]{0:T(1024)S(1)}, f32[768]{0:T(1024)}, u32[]{:S(2)}) copy-start(f32[768]{0:T(1024)} %param.17) | copy-start | bytes 9220
  233.4 2.6 copy-start.9
  550.9 4.2 copy-start.24
  550.9 5.2 copy-start.11
  555.1 4.2 slice-start.2
  556.1 3.4 slice-start.3
  559.5 3.4 copy-start.1
Sparse Core Ops, SparseCore 0:
  24.8 23.0 all-reduce.7
  66.6 21.5 all-reduce.9
  124.7 24.5 all-reduce.13
  156.7 394.1 all-reduce.11
where the time goes:
time: 570 us; the launch traced here: 569 us
  waiting for transfers between devices  358 us (63%)
  blocking collectives  81.9 us (14%)
  matrix products  56.4 us (10%)
  other arithmetic  34.4 us (6%)
  local copies, waits for them, and re-layouts  23.9 us (4%)
  between operations  14.4 us (3%)
    psum x1, waiting for transfers between devices, body(): lax.psum((grad_attention_gain, grad_attention_shift, grad_packed_weight,...  312 us
    psum x1, blocking collectives, body(): lax.psum((grad_attention_gain, grad_attention_shift, grad_packed_weight,...  81.9 us
    psum x1, waiting for transfers between devices, body(): lax.psum(jnp.dot(attended, output_weight, preferred_element_type=jnp.floa...  23.2 us
    unnamed x118, local copies, waits for them, and re-layouts  21.4 us
    psum x1, waiting for transfers between devices, body(): lax.psum(lax.dot_general(grad_pre, expand_weight, contract_cols, preferre...  14.2 us
  transfers between devices with their start and end apart: 4, of which 4 were waited for; matrix products, arithmetic and copies ran while one was open for 5% of the time, Pallas kernels for 0%

commit v1 on v0

--- a/solution.py
+++ b/solution.py
@@ -1,11 +1,345 @@
+import functools
 import math
 
 import jax
 import jax.numpy as jnp
 from jax import lax
+from jax.experimental import pallas as pl
+from jax.experimental.pallas import tpu as pltpu
 from jax.sharding import PartitionSpec as P
 
 HEAD = 64
+
+
+MESH = pl.DeviceIdType.MESH
+W = 8
+R = 64
+LF = 2
+
+
+class Comm:
+    def __init__(self, n, counts, G, O, RF, RU, RD, RL, sems):
+        self.nz = n // 4
+        self.counts = counts
+        self.G, self.O, self.RF, self.RU, self.RD, self.RL = G, O, RF, RU, RD, RL
+        self.sems = sems
+        d = lax.axis_index("dp")
+        self.t = lax.axis_index("tensor")
+        self.d = d
+        self.z = d // 4
+        self.y = (d // 2) % 2
+        self.x = d % 2
+        self.px = d + 1 - 2 * self.x
+        self.py = d + 2 - 4 * self.y
+
+    def steps(self):
+        return max(self.counts) + LF + 2 * self.nz + 3
+
+    def barrier(self):
+        b = pltpu.get_barrier_semaphore()
+        for peer in (self.px, self.py):
+            pl.semaphore_signal(b, inc=1, device_id=(peer, self.t), device_id_type=MESH)
+
+        @pl.when(self.z > 0)
+        def _():
+            pl.semaphore_signal(b, inc=1, device_id=(self.d - 4, self.t), device_id_type=MESH)
+
+        @pl.when(self.z < self.nz - 1)
+        def _():
+            pl.semaphore_signal(b, inc=1, device_id=(self.d + 4, self.t), device_id_type=MESH)
+
+        edge = (self.z > 0).astype(jnp.int32) + (self.z < self.nz - 1).astype(jnp.int32)
+        pl.semaphore_wait(b, 2 + edge)
+
+    def rows(self, start, size):
+        return self.G.at[pl.ds(pl.multiple_of(start, 8), size), :]
+
+    def done(self, start, size):
+        return self.O.at[pl.ds(pl.multiple_of(start, 8), size), :]
+
+    def copy(self, src, dst, kind, idx, dev):
+        return pltpu.make_async_remote_copy(
+            src_ref=src, dst_ref=dst, send_sem=self.sems[kind + "s"].at[idx], recv_sem=self.sems[kind + "r"].at[idx],
+            device_id=(dev, self.t), device_id_type=MESH)
+
+    def add(self, start, size, buf):
+        r = self.rows(start, size)
+        r[...] = r[...] + buf[...]
+
+    def step(self, i):
+        for c in (0, 1):
+            self.first(c, i)
+        for c in (0, 1):
+            self.rest(c, i)
+
+    def base(self, c, k):
+        return (2 * k + c) * R
+
+    def f_copy(self, c, k):
+        a, dev = (self.x, self.px) if c == 0 else (self.y, self.py)
+        q = k % W
+        return self.copy(self.rows(self.base(c, k) + (1 - a) * (R // 2), R // 2), self.RF.at[c, q], "F", (c, q), dev)
+
+    def first(self, c, i):
+        @pl.when(i < self.counts[c])
+        def _():
+            self.f_copy(c, i).start()
+
+    def rest(self, c, i):
+        nz, z = self.nz, self.z
+        a, fdev, b, ldev = (self.x, self.px, self.y, self.py) if c == 0 else (self.y, self.py, self.x, self.px)
+        n = self.counts[c]
+        H, Q, E = R // 2, R // 4, R // 8
+
+        def ok(k):
+            return (k >= 0) & (k < n)
+
+        def half(k):
+            return self.base(c, k) + a * H
+
+        def sub(k, s):
+            return half(k) + s * Q
+
+        def root(k, s):
+            return k % 2 if s == 0 else nz - 1 - k % 2
+
+        k = i - LF
+
+        @pl.when(ok(k))
+        def _(k=k):
+            cp = self.f_copy(c, k)
+            cp.wait_send()
+            cp.wait_recv()
+            self.add(half(k), H, self.RF.at[c, k % W])
+
+        def up(k, s):
+            return self.copy(self.rows(sub(k, s), Q), self.RU.at[c, s, k % W], "U", (c, s, k % W), jnp.minimum(self.d + 4, 4 * nz - 1))
+
+        def dn(k, s):
+            return self.copy(self.rows(sub(k, s), Q), self.RD.at[c, s, k % W], "D", (c, s, k % W), jnp.maximum(self.d - 4, 0))
+
+        for s in (0, 1):
+            k = i - (LF + z)
+
+            @pl.when(ok(k) & (z <= root(k, s)) & (z > 0))
+            def _(k=k, s=s):
+                up(k, s).wait_recv()
+                self.add(sub(k, s), Q, self.RU.at[c, s, k % W])
+
+            @pl.when(ok(k) & (z < root(k, s)))
+            def _(k=k, s=s):
+                up(k, s).start()
+
+            k = i - (LF + nz - 1 - z)
+
+            @pl.when(ok(k) & (z >= root(k, s)) & (z < nz - 1))
+            def _(k=k, s=s):
+                dn(k, s).wait_recv()
+                self.add(sub(k, s), Q, self.RD.at[c, s, k % W])
+
+            @pl.when(ok(k) & (z > root(k, s)))
+            def _(k=k, s=s):
+                dn(k, s).start()
+
+            k = i - (LF + z + 1)
+
+            @pl.when(ok(k) & (z < root(k, s)))
+            def _(k=k, s=s):
+                up(k, s).wait_send()
+
+            k = i - (LF + nz - 1 - z + 1)
+
+            @pl.when(ok(k) & (z > root(k, s)))
+            def _(k=k, s=s):
+                dn(k, s).wait_send()
+
+        def last(k, s):
+            return self.copy(self.rows(sub(k, s) + (1 - b) * E, E), self.RL.at[c, k % W], "L", (c, k % W), ldev)
+
+        def last_back(k, s):
+            at = sub(k, s) + b * E
+            return self.copy(self.rows(at, E), self.done(at, E), "M", (c, k % W), ldev)
+
+        for s in (0, 1):
+            k = i - (LF + nz - 1)
+
+            @pl.when(ok(k) & (z == root(k, s)))
+            def _(k=k, s=s):
+                last(k, s).start()
+
+            k = i - (LF + nz)
+
+            @pl.when(ok(k) & (z == root(k, s)))
+            def _(k=k, s=s):
+                cp = last(k, s)
+                cp.wait_send()
+                cp.wait_recv()
+                self.add(sub(k, s) + b * E, E, self.RL.at[c, k % W])
+                last_back(k, s).start()
+                self.done(sub(k, s) + b * E, E)[...] = self.rows(sub(k, s) + b * E, E)[...]
+
+        def g_up(k, s):
+            r = self.done(sub(k, s), Q)
+            return self.copy(r, r, "V", (c, s, k % W), jnp.minimum(self.d + 4, 4 * nz - 1))
+
+        def g_dn(k, s):
+            r = self.done(sub(k, s), Q)
+            return self.copy(r, r, "E", (c, s, k % W), jnp.maximum(self.d - 4, 0))
+
+        def g_first(k, s):
+            r = self.done(sub(k, s), Q)
+            return self.copy(r, r, "G", (c, s, k % W), fdev)
+
+        for e in (0, 1):
+            for s in (0, 1):
+                r = e if s == 0 else nz - 1 - e
+                lag = LF + nz + 1 + jnp.abs(z - r)
+                k = i - lag
+                here = ok(k) & (k % 2 == e)
+
+                @pl.when(here & (z == r))
+                def _(k=k, s=s):
+                    cp = last_back(k, s)
+                    cp.wait_send()
+                    cp.wait_recv()
+
+                @pl.when(here & (z < r))
+                def _(k=k, s=s):
+                    g_dn(k, s).wait_recv()
+
+                @pl.when(here & (z > r))
+                def _(k=k, s=s):
+                    g_up(k, s).wait_recv()
+
+                @pl.when(here & (z <= r) & (z > 0))
+                def _(k=k, s=s):
+                    g_dn(k, s).start()
+
+                @pl.when(here & (z >= r) & (z < nz - 1))
+                def _(k=k, s=s):
+                    g_up(k, s).start()
+
+                @pl.when(here)
+                def _(k=k, s=s):
+                    g_first(k, s).start()
+
+                k = i - (lag + 1)
+                here = ok(k) & (k % 2 == e)
+
+                @pl.when(here)
+                def _(k=k, s=s):
+                    cp = g_first(k, s)
+                    cp.wait_send()
+                    cp.wait_recv()
+
+                @pl.when(here & (z <= r) & (z > 0))
+                def _(k=k, s=s):
+                    g_dn(k, s).wait_send()
+
+                @pl.when(here & (z >= r) & (z < nz - 1))
+                def _(k=k, s=s):
+                    g_up(k, s).wait_send()
+
+
+KINDS = {"F": (2, W), "U": (2, 2, W), "D": (2, 2, W), "L": (2, W), "M": (2, W), "V": (2, 2, W), "E": (2, 2, W), "G": (2, 2, W)}
+SEMS = [k + e for k in KINDS for e in "sr"]
+
+
+def comm_scratch(width):
+    return [
+        pltpu.VMEM((2, W, R // 2, width), jnp.float32),
+        pltpu.VMEM((2, 2, W, R // 4, width), jnp.float32),
+        pltpu.VMEM((2, 2, W, R // 4, width), jnp.float32),
+        pltpu.VMEM((2, W, R // 8, width), jnp.float32),
+    ] + [pltpu.SemaphoreType.DMA(KINDS[k[0]]) for k in SEMS]
+
+
+def pieces_of(width, hidden, heads_width):
+    out = []
+    row = 0
+    out.append((row, 0, 0, 0, hidden, width, 0))
+    row += hidden
+    for part in range(hidden // width):
+        out.append((row, 1, 0, part * width, width, width, 0))
+        row += width
+    out.append((row, 2, 0, 0, heads_width, width, 0))
+    row += heads_width
+    for part in range(2):
+        out.append((row, 3, 0, part * heads_width, width, heads_width, part * heads_width))
+    row += width
+    for part in range(2):
+        out.append((row, 3, part * heads_width, 2 * heads_width, heads_width, heads_width, part * heads_width))
+    row += heads_width
+    out.append((row, 4, 0, 0, R, width, 0))
+    row += R
+    return out, row
+
+
+def moves(arrays, whole, blocks, local, out):
+    made = []
+    for j, (row, which, r0, c0, nr, nc, g0) in enumerate(blocks):
+        here = whole.at[pl.ds(row, nr), pl.ds(g0, nc)]
+        there = arrays[which]
+        if len(there.shape) == 3:
+            there = there.at[c0 // nc]
+            c0 = 0
+        there = there.at[pl.ds(r0, nr), pl.ds(c0, nc)]
+        pair = (here, there) if out else (there, here)
+        made.append(pltpu.make_async_copy(*pair, local.at[j]))
+    return made
+
+
+def sum_kernel(n, blocks, total, *refs):
+    ins, O = refs[:5], refs[5]
+    G, RF, RU, RD, RL, local = refs[6:12]
+    sems = dict(zip(SEMS, refs[12:]))
+    full = (total - R) // (2 * R)
+    comm = Comm(n, (full + 1, full), G, O, RF, RU, RD, RL, sems)
+    loads = moves(ins, G, blocks, local, False)
+    for cp in loads:
+        cp.start()
+    comm.barrier()
+    for cp in loads:
+        cp.wait()
+
+    def body(i, carry):
+        comm.step(i)
+        return carry
+
+    lax.fori_loop(0, comm.steps(), body, 0)
+
+
+def unpack_kernel(blocks, whole, *refs):
+    stores = moves(refs[:5], whole, blocks, refs[5], True)
+    for cp in stores:
+        cp.start()
+    for cp in stores:
+        cp.wait()
+
+
+def sum_grads(n, arrays, width, hidden, heads_width):
+    blocks, total = pieces_of(width, hidden, heads_width)
+    anywhere = pl.BlockSpec(memory_space=pl.ANY)
+    scratch = comm_scratch(width)
+    local = pltpu.SemaphoreType.DMA((len(blocks),))
+    summed = pl.pallas_call(
+        functools.partial(sum_kernel, n, blocks, total),
+        out_shape=pltpu.VMEM((total, width), jnp.float32),
+        in_specs=[anywhere] * 5,
+        out_specs=pl.BlockSpec(memory_space=pltpu.VMEM),
+        scratch_shapes=[pltpu.VMEM((total, width), jnp.float32)] + scratch[:4] + [local] + scratch[4:],
+        compiler_params=pltpu.CompilerParams(
+            collective_id=0, has_side_effects=True, vmem_limit_bytes=26 << 20
+        ),
+    )(*arrays)
+    return pl.pallas_call(
+        functools.partial(unpack_kernel, blocks),
+        out_shape=[pltpu.HBM(a.shape, jnp.float32) for a in arrays],
+        in_specs=[anywhere],
+        out_specs=[anywhere] * 5,
+        scratch_shapes=[local],
+        compiler_params=pltpu.CompilerParams(vmem_limit_bytes=1 << 20),
+    )(summed)
 
 
 EPSILON = 1e-05
@@ -67,6 +401,7 @@
 
 
 def body(
+    n_dp,
     block_input,
     sequence_ids,
     attention_gain,
@@ -189,38 +524,55 @@
     grad_input = (
         grad_middle + norm_back(grad_attend_in, normed_a, inv_std_a, attention_gain)
     ).astype(jnp.bfloat16)
-    every_grad = lax.psum(
-        (
-            grad_attention_gain,
-            grad_attention_shift,
-            grad_packed_weight,
-            grad_packed_bias,
+    width = block_input.shape[1]
+    hidden = expand_weight.shape[1]
+    small = [
+        grad_attention_gain,
+        grad_attention_shift,
+        grad_packed_bias.reshape(-1),
+        grad_output_bias,
+        grad_feedforward_gain,
+        grad_feedforward_shift,
+        grad_expand_bias,
+        grad_shrink_bias,
+    ]
+    sizes = [a.size for a in small]
+    flat = jnp.concatenate(small)
+    flat = jnp.pad(flat, (0, R * width - flat.size)).reshape(R, width)
+    shrink_sum, expand_sum, output_sum, packed_sum, flat = sum_grads(
+        n_dp,
+        [
+            grad_shrink_weight,
+            grad_expand_weight,
             grad_output_weight,
-            grad_output_bias,
-            grad_feedforward_gain,
-            grad_feedforward_shift,
-            grad_expand_weight,
-            grad_expand_bias,
-            grad_shrink_weight,
-            grad_shrink_bias,
-        ),
-        "dp",
-    )
+            jnp.transpose(grad_packed_weight, (1, 0, 2)),
+            flat,
+        ],
+        width,
+        hidden,
+        local_width,
+    )
+    flat = flat.reshape(-1)
+    parts = []
+    place = 0
+    for size in sizes:
+        parts.append(flat[place : place + size])
+        place += size
     return (
         block_output,
         grad_input,
-        every_grad[0],
-        every_grad[1],
-        every_grad[2],
-        every_grad[3],
-        every_grad[4],
-        every_grad[5],
-        every_grad[6],
-        every_grad[7],
-        every_grad[8],
-        every_grad[9],
-        every_grad[10],
-        every_grad[11],
+        parts[0],
+        parts[1],
+        jnp.transpose(packed_sum, (1, 0, 2)),
+        parts[2].reshape(3, local_width),
+        output_sum,
+        parts[3],
+        parts[4],
+        parts[5],
+        expand_sum,
+        parts[6],
+        shrink_sum,
+        parts[7],
     )
 
 
@@ -258,4 +610,5 @@
         P("tensor", None),
         P(),
     )
-    return jax.shard_map(body, mesh=mesh, in_specs=in_specs, out_specs=out_specs, check_vma=False)
+    return jax.shard_map(
+        functools.partial(body, mesh.shape["dp"]), mesh=mesh, in_specs=in_specs, out_specs=out_specs, check_vma=False)

time: 570 us -> 389 us (0.68)
  waiting for transfers between devices: 358 us -> 45.5 us
  Pallas kernels: 0 us -> 212 us
  blocking collectives: 81.9 us -> 0 us
    psum x1 -> x0, waiting for transfers between devices: 312 us -> none  [body(): lax.psum((grad_attention_gain, grad_attention_shift, grad_packed_weight,...]
    pallas_call x0 -> x2, Pallas kernels: none -> 212 us  [the longest x1 206 us: sum_grads(): pl.pallas_call(functools.partial(sum_kernel, n, blocks, total), out_shape...]
    psum x1 -> x0, blocking collectives: 81.9 us -> none  [body(): lax.psum((grad_attention_gain, grad_attention_shift, grad_packed_weight,...]
    unnamed x118 -> x115, local copies, waits for them, and re-layouts: 21.4 us -> 15.4 us
  transfers between devices with their start and end apart: 4 -> 3, of which waited for: 4 -> 3; matrix products, arithmetic and copies ran while one was open for 5% -> 6% of each run, Pallas kernels for 0% -> 0%
where the time goes in v1:
time: 389 us; the launch traced here: 388 us
  Pallas kernels  212 us (54%)
  matrix products  58 us (15%)
  waiting for transfers between devices  45.5 us (12%)
  other arithmetic  35.2 us (9%)
  local copies, waits for them, and re-layouts  23.1 us (6%)
  between operations  14.5 us (4%)
    pallas_call x1, Pallas kernels, sum_grads(): pl.pallas_call(functools.partial(sum_kernel, n, blocks, total), out_shape...  206 us
    psum x1, waiting for transfers between devices, body(): lax.psum(jnp.dot(attended, output_weight, preferred_element_type=jnp.floa...  23.2 us
    unnamed x115, local copies, waits for them, and re-layouts  15.4 us
    psum x1, waiting for transfers between devices, body(): lax.psum(lax.dot_general(grad_pre, expand_weight, contract_cols, preferre...  14.2 us
    dot_general x1, matrix products, body(): lax.dot_general(grad_output, shrink_weight, contract_cols, preferred_elem...  10.1 us
    psum x1, waiting for transfers between devices, body(): lax.psum(jnp.dot(act_low, shrink_weight, preferred_element_type=jnp.float...  8.08 us
  transfers between devices with their start and end apart: 3, of which 3 were waited for; matrix products, arithmetic and copies ran while one was open for 6% of the time, Pallas kernels for 0%

profile of v1, /device:TPU:0, one launch (start us, length us, event | category | flops | bytes accessed | tf_op | source)
XLA Modules:
  0.0 388.1 jit_solution(3482061584737728900)
XLA Ops:
  7.3 1.1 broadcast_compare_fusion
  8.3 0.9 convert_reduce_fusion.4
  9.3 1.3 convert_reduce_fusion.1
  10.6 1.5 fusion.22
  12.1 3.0 convolution_add_fusion.1
  15.3 0.3 multiply_cosine_fusion
  15.6 0.3 subtract_convert_fusion.3
  15.9 0.6 copy-done.32
  16.6 1.2 fusion
  17.8 1.3 exponential_reduce_fusion
  19.2 1.3 copy-done.5
  20.5 1.7 convolution_convert_fusion.2
  22.3 0.7 copy-done.18
  23.0 1.7 fusion.48
  24.8 23.2 %all-reduce.6.cloned.1.call-done = f32[512,768]{1,0:T(8,128)} async-done(((f32[512,768]{1,0:T(8,128)}), f32[512,768]{1,0:T(8,128)}) %all-reduce.6.cloned.1.call-update) | async-done | bytes 1572880 | tf_op jit(solution)/shard_map/psum | solution.py:451
  48.0 1.8 fusion.45
  49.8 0.3 multiply_reduce_fusion.3
  50.2 0.8 copy-done.6
  51.0 1.5 convolution_add_fusion
  52.5 10.1 %convert_reduce_fusion = (f32[1536]{0:T(1024)}, bf16[512,1536]{1,0:T(8,128)(2,1)S(1)}, f32[512,1536]{1,0:T(8,128)}) fusion(f32[512,1536]{1,0:T(8,128)S(1)} %convolution_add_fusion, bf16[512,768]{1,0:T(8,128)(2,1)S(1)} %copy-done.13, bf16[1536,768]{1,0:T(8,128)(2,1)S(1)} %copy-done), kind=kOutput, calls=%fused_computation.10 | convolution fusion | flops 1266153984 | bytes 11016192 | tf_op jit(solution)/shard_map/dot_general | solution.py:465
  62.7 1.2 copy-done.50
  63.8 2.6 fusion.50
  66.5 0.2 all-reduce.10.cloned.1.call-start
  66.7 3.6 multiply_convert_fusion.1
  70.3 1.1 copy-done.10
  71.4 2.5 fusion.49
  74.0 14.2 %all-reduce.8.cloned.1.call-done = f32[512,768]{1,0:T(8,128)} async-done(((f32[512,768]{1,0:T(8,128)}), f32[512,768]{1,0:T(8,128)}) %all-reduce.8.cloned.1.call-update) | async-done | bytes 1572880 | tf_op jit(solution)/shard_map/psum | solution.py:473
  88.2 3.3 multiply_reduce_fusion.1
  91.5 2.5 fusion.44
  94.0 1.2 copy-done.8
  95.3 0.5 convolution_convert_fusion.1
  95.8 5.5 %convolution_convert_fusion = bf16[6,64,512]{2,1,0:T(8,128)(2,1)} fusion(bf16[512,6,64]{0,2,1:T(8,128)(2,1)S(1)} %bitcast.59, f32[6,512,512]{1,2,0:T(8,128)} %copy-done.5, f32[6,512]{1,0:T(8,128)S(1)} %log_add_fusion, pred[512,512]{0,1:T(8,128)(4,1)S(1)} %broadcast_compare_fusion), kind=kOutput, calls=%fused_computation.63 | convolution fusion | flops 207814656 | bytes 7352320 | tf_op jit(solution)/shard_map/hqk,qhd->khd/dot_general | solution.py:494
  101.3 5.8 %multiply_reduce_fusion = (f32[6,512]{1,0:T(8,128)S(1)}, f32[6,512,512]{1,2,0:T(8,128)}) fusion(f32[6,512,512]{1,2,0:T(8,128)S(1)} %bitcast.55, f32[6,512]{1,0:T(8,128)S(1)} %log_add_fusion, pred[512,512]{0,1:T(8,128)(4,1)S(1)} %broadcast_compare_fusion, bf16[512,6,64]{0,2,1:T(8,128)(2,1)S(1)} %bitcast.60, f32[512,3,6,64]{0,3,2,1:T(8,128)} %bitcast.58), kind=kOutput, calls=%fused_computation.1 | convolution fusion | flops 209187840 | bytes 13656064 | tf_op jit(solution)/shard_map/qhd,khd->hqk/dot_general | solution.py:489
  107.1 4.7 %multiply_convert_fusion = bf16[6,512,512]{1,2,0:T(8,128)(2,1)S(1)} fusion(f32[6,512,512]{1,2,0:T(8,128)} %get-tuple-element.67, f32[6,512,512]{1,2,0:T(8,128)S(1)} %bitcast.55, f32[6,512]{1,0:T(8,128)S(1)} %get-tuple-element.66, f32[6,512]{1,0:T(8,128)S(1)} %log_add_fusion, pred[512,512]{0,1:T(8,128)(4,1)S(1)} %broadcast_compare_fusion), kind=kLoop, calls=%fused_computation | loop fusion | flops 9437184 | bytes 16015360 | tf_op jit(solution)/shard_map/convert_element_type | solution.py:493
  111.8 0.6 fusion.25
  112.5 0.3 copy-done.25
  112.8 1.9 fusion.24
  114.8 1.2 copy.36
  116.0 2.2 add_convert_fusion.4
  118.2 0.2 copy.35
  118.5 1.2 pad_maximum_fusion.3
  119.7 0.9 copy.34
  120.6 4.0 %convolution_bitcast_fusion.1 = f32[512,768]{1,0:T(8,128)} fusion(bf16[768,3,384]{2,0,1:T(8,128)(2,1)} %param.19, bf16[512,1,384]{2,0,1:T(8,128)(2,1)S(1)} %copy.36, bf16[512,1,384]{2,0,1:T(8,128)(2,1)S(1)} %copy.35, bf16[512,1,384]{2,0,1:T(8,128)(2,1)} %copy.34), kind=kOutput, calls=%fused_computation.55 | convolution fusion | flops 907149312 | bytes 4521984 | tf_op jit(solution)/shard_map/tcw,dcw->td/dot_general | solution.py:519
  124.6 1.1 copy-done.14
  125.7 5.4 %fusion.51.refs_0_ = f32[1536,768]{1,0:T(8,128)} fusion(bf16[512,1536]{1,0:T(8,128)(2,1)} %copy-done.10, bf16[512,768]{1,0:T(8,128)(2,1)S(1)} %copy-done.14), kind=kOutput, calls=%fused_computation.124 | convolution fusion | flops 1207959552 | bytes 7077888 | tf_op jit(solution)/shard_map/dot_general | solution.py:462
  131.1 3.8 fusion.42.refs_1_
  135.0 0.2 convert_reduce_fusion.2
  135.2 2.0 fusion.28.refs_2_
  137.2 3.9 %convolution_bitcast_fusion.refs_3_ = f32[3,768,384]{2,1,0:T(8,128)} fusion(bf16[512,768]{1,0:T(8,128)(2,1)S(1)} %copy-done.9, f32[768]{0:T(1024)} %param.18, f32[768]{0:T(1024)} %param.17, f32[512]{0:T(512)S(1)} %add_rsqrt_fusion.1, f32[512]{0:T(512)S(1)} %broadcast_multiply_fusion.5, bf16[512,1,384]{2,0,1:T(8,128)(2,1)S(1)} %copy.36, ...), kind=kOutput, calls=%fused_computation.30 | convolution fusion | flops 911867904 | bytes 5515264 | tf_op jit(solution)/shard_map/td,tcw->dcw/dot_general | solution.py:515
  141.2 8.1 %all-reduce.10.cloned.1.call-done = (f32[512,768]{1,0:T(8,128)}, f32[512,768]{1,0:T(8,128)}) async-done(((f32[512,768]{1,0:T(8,128)}, f32[512,768]{1,0:T(8,128)}), (f32[512,768]{1,0:T(8,128)}, f32[512,768]{1,0:T(8,128)})) %all-reduce.10.cloned.1.call-update) | async-done | bytes 3145744 | tf_op jit(solution)/shard_map/psum | solution.py:458
  149.3 2.2 fusion.21
  151.7 2.3 copy-done.2
  154.1 2.3 copy-done.3
  156.4 2.0 copy-done.4
  158.4 206.4 %shard_map.254.whole = f32[4672,768]{1,0:T(8,128)S(1)} custom-call(f32[1536,768]{1,0:T(8,128)S(1)} %copy-done.2, f32[768,1536]{1,0:T(8,128)S(1)} %copy-done.3, f32[384,768]{1,0:T(8,128)S(1)} %fusion.28.refs_2_, f32[3,768,384]{2,1,0:T(8,128)S(1)} %copy-done.4, f32[64,768]{1,0:T(8,128)S(1)} %reshape.208.refs_4_), custom_call_target="tpu_custom_call" | custom-call | tf_op jit(solution)/shard_map/pallas_call | solution.py:325
  364.8 5.2 %shard_map.255 = (f32[1536,768]{1,0:T(8,128)}, f32[768,1536]{1,0:T(8,128)}, f32[384,768]{1,0:T(8,128)}, f32[3,768,384]{2,1,0:T(8,128)}, f32[64,768]{1,0:T(8,128)}) custom-call(f32[4672,768]{1,0:T(8,128)S(1)} %shard_map.254.whole), custom_call_target="tpu_custom_call" | custom-call | tf_op jit(solution)/shard_map/pallas_call | solution.py:335
  370.0 1.4 slice_reduce_fusion
  371.4 1.0 slice.82
  372.4 0.9 reshape.209
  373.3 0.6 fusion.47
  373.9 0.6 slice.104
  374.5 0.6 slice.100
  375.1 3.1 add_convert_fusion.1
  378.3 3.3 fusion.20
  (126 shorter events, 0.8 us)
Async XLA Ops:
  7.2 45.3 %copy-start = (bf16[1536,768]{1,0:T(8,128)(2,1)S(1)}, bf16[1536,768]{1,0:T(8,128)(2,1)}, u32[]{:S(2)}) copy-start(bf16[1536,768]{1,0:T(8,128)(2,1)} %param.27) | copy-start | bytes 7077892
  7.2 40.8 %all-reduce.6.cloned.1.call-start = ((), (), s32[]{:S(2)}) async-start(), calls=%async_computation | async-start | bytes 3145728 | tf_op jit(solution)/shard_map/psum | solution.py:451
  15.1 4.0 %copy-start.17 = (f32[512,3,384]{0,2,1:T(8,128)}, f32[512,3,384]{0,2,1:T(8,128)S(1)}, u32[]{:S(2)}) copy-start(f32[512,3,384]{0,2,1:T(8,128)S(1)} %convolution_add_fusion.1) | copy-start | bytes 7077892
  15.6 0.9 copy-start.32
  15.6 0.9 copy-start.33
  15.9 1.9 copy-start.24
  15.9 1.9 copy-start.26
  15.9 1.9 copy-start.28
  15.9 1.9 copy-start.30
  17.8 2.7 copy-start.5
  20.5 2.5 copy-start.15
  22.2 0.7 copy-start.18
  22.2 25.8 %copy-start.9 = (bf16[512,768]{1,0:T(8,128)(2,1)S(1)}, bf16[512,768]{1,0:T(8,128)(2,1)}, u32[]{:S(2)}) copy-start(bf16[512,768]{1,0:T(8,128)(2,1)} %param.15) | copy-start | bytes 2359300
  22.2 25.7 %copy-start.45 = (f32[768]{0:T(1024)S(1)}, f32[768]{0:T(1024)}, u32[]{:S(2)}) copy-start(f32[768]{0:T(1024)} %param.22) | copy-start | bytes 9220
  24.7 26.2 %copy-start.35 = (f32[768]{0:T(1024)S(1)}, f32[768]{0:T(1024)}, u32[]{:S(2)}) copy-start(f32[768]{0:T(1024)} %param.23) | copy-start | bytes 9220
  24.7 26.2 %copy-start.47 = (f32[1536]{0:T(1024)S(1)}, f32[1536]{0:T(1024)}, u32[]{:S(2)}) copy-start(f32[1536]{0:T(1024)} %param.26) | copy-start | bytes 18436
  24.8 26.2 %copy-start.48 = (f32[768]{0:T(1024)S(1)}, f32[768]{0:T(1024)}, u32[]{:S(2)}) copy-start(f32[768]{0:T(1024)} %param.24) | copy-start | bytes 9220
  24.8 63.4 %all-reduce.8.cloned.1.call-start = ((), (), s32[]{:S(2)}) async-start(), calls=%async_computation.1 | async-start | bytes 3145728 | tf_op jit(solution)/shard_map/psum | solution.py:473
  48.0 3.0 copy-start.46
  49.8 1.1 copy-start.6
  51.0 1.5 copy-start.13
  52.5 10.1 %copy-start.12 = (f32[512,1536]{1,0:T(8,128)}, f32[512,1536]{1,0:T(8,128)S(1)}, u32[]{:S(2)}) copy-start(f32[512,1536]{1,0:T(8,128)S(1)} %convolution_add_fusion) | copy-start | bytes 9437188
  62.7 1.2 copy-start.50
  66.5 82.8 %all-reduce.10.cloned.1.call-start = ((), (), s32[]{:S(2)}) async-start(), calls=%async_computation.2 | async-start | bytes 6291456 | tf_op jit(solution)/shard_map/psum | solution.py:458
  70.3 1.1 copy-start.10
  74.0 17.5 %copy-start.7 = (f32[512,768]{1,0:T(8,128)S(1)}, f32[512,768]{1,0:T(8,128)}, u32[]{:S(2)}) copy-start(f32[512,768]{1,0:T(8,128)} %copy-done.6) | copy-start | bytes 4718596
  88.2 3.3 copy-start.11
  91.5 3.8 copy-start.16
  94.0 1.2 copy-start.8
  95.3 6.0 %slice-start = ((s8[6291456]{0:T(1024)(128)(4,1)}), s8[4194304]{0:T(1024)(128)(4,1)S(1)}, s32[]{:S(2)}) async-start(s8[6291456]{0:T(1024)(128)(4,1)} %bitcast.54), calls=%async_computation.3 | async-start | bytes 8388608
  95.8 5.5 %slice-start.1 = ((s8[6291456]{0:T(1024)(128)(4,1)}), s8[2097152]{0:T(1024)(128)(4,1)S(1)}, s32[]{:S(2)}) async-start(s8[6291456]{0:T(1024)(128)(4,1)} %bitcast.54), calls=%async_computation.4 | async-start | bytes 4194304
  107.1 4.8 %copy-start.29 = (bf16[512,6,32]{0,2,1:T(8,128)(2,1)S(1)}, bf16[512,6,32]{0,2,1:T(8,128)(2,1)}, u32[]{:S(2)}) copy-start(bf16[512,6,32]{0,2,1:T(8,128)(2,1)} %copy-done.28) | copy-start | bytes 589828
  107.1 4.8 %copy-start.31 = (bf16[512,6,32]{0,2,1:T(8,128)(2,1)S(1)}, bf16[512,6,32]{0,2,1:T(8,128)(2,1)}, u32[]{:S(2)}) copy-start(bf16[512,6,32]{0,2,1:T(8,128)(2,1)} %copy-done.30) | copy-start | bytes 589828
  111.8 0.9 copy-start.25
  111.8 1.0 copy-start.27
  118.4 2.1 copy-start.20
  124.6 1.1 copy-start.14
  125.7 5.4 %copy-start.36 = (f32[768]{0:T(1024)S(1)}, f32[768]{0:T(1024)}, u32[]{:S(2)}) copy-start(f32[768]{0:T(1024)} %param.23) | copy-start | bytes 9220
  125.7 5.4 %copy-start.49 = (f32[768]{0:T(1024)S(1)}, f32[768]{0:T(1024)}, u32[]{:S(2)}) copy-start(f32[768]{0:T(1024)} %param.24) | copy-start | bytes 9220
  125.7 5.4 %copy-start.51 = (bf16[512,1536]{1,0:T(8,128)(2,1)S(1)}, bf16[512,1536]{1,0:T(8,128)(2,1)}, u32[]{:S(2)}) copy-start(bf16[512,1536]{1,0:T(8,128)(2,1)} %copy-done.50) | copy-start | bytes 4718596
  131.1 3.9 copy-start.21
  131.1 3.9 copy-start.22
  131.1 4.1 %copy-start.19 = (bf16[6,64,512]{2,1,0:T(8,128)(2,1)S(1)}, bf16[6,64,512]{2,1,0:T(8,128)(2,1)}, u32[]{:S(2)}) copy-start(bf16[6,64,512]{2,1,0:T(8,128)(2,1)} %copy-done.18) | copy-start | bytes 1179652
  135.0 2.2 copy-start.23
  137.2 12.1 %copy-start.41 = (f32[768]{0:T(1024)S(1)}, f32[768]{0:T(1024)}, u32[]{:S(2)}) copy-start(f32[768]{0:T(1024)} %param.17) | copy-start | bytes 9220
  141.2 10.3 %copy-start.34 = (f32[7296]{0:T(1024)S(1)}, f32[7296]{0:T(1024)}, u32[]{:S(2)}) copy-start(f32[7296]{0:T(1024)} %custom-call) | copy-start | bytes 87556
  141.2 10.4 %copy-start.40 = (f32[768]{0:T(1024)S(1)}, f32[768]{0:T(1024)}, u32[]{:S(2)}) copy-start(f32[768]{0:T(1024)} %get-tuple-element.39) | copy-start | bytes 9220
  141.2 10.4 %copy-start.39 = (f32[768]{0:T(1024)S(1)}, f32[768]{0:T(1024)}, u32[]{:S(2)}) copy-start(f32[768]{0:T(1024)} %get-tuple-element.24) | copy-start | bytes 9220
  141.2 10.4 %copy-start.37 = (f32[768]{0:T(1024)S(1)}, f32[768]{0:T(1024)}, u32[]{:S(2)}) copy-start(f32[768]{0:T(1024)} %get-tuple-element.30) | copy-start | bytes 9220
  141.2 10.4 %copy-start.43 = (f32[1536]{0:T(1024)S(1)}, f32[1536]{0:T(1024)}, u32[]{:S(2)}) copy-start(f32[1536]{0:T(1024)} %get-tuple-element.36) | copy-start | bytes 18436
  141.2 10.4 %copy-start.38 = (f32[768]{0:T(1024)S(1)}, f32[768]{0:T(1024)}, u32[]{:S(2)}) copy-start(f32[768]{0:T(1024)} %get-tuple-element.53) | copy-start | bytes 9220
  151.7 2.3 copy-start.2
  154.0 2.3 copy-start.3
  156.4 2.0 copy-start.4
  364.8 10.3 %copy-start.44 = (f32[768]{0:T(1024)S(1)}, f32[768]{0:T(1024)}, u32[]{:S(2)}) copy-start(f32[768]{0:T(1024)} %param.28) | copy-start | bytes 9220
  371.4 6.9 %copy-start.42 = (f32[768]{0:T(1024)S(1)}, f32[768]{0:T(1024)}, u32[]{:S(2)}) copy-start(f32[768]{0:T(1024)} %param.17) | copy-start | bytes 9220
  375.1 6.4 %copy-start.1 = (bf16[1536,768]{1,0:T(8,128)(2,1)S(1)}, bf16[1536,768]{1,0:T(8,128)(2,1)}, u32[]{:S(2)}) copy-start(bf16[1536,768]{1,0:T(8,128)(2,1)} %param.27) | copy-start | bytes 7077892
Sparse Core Ops, SparseCore 0:
  24.9 23.0 all-reduce.5
  66.6 21.5 all-reduce.7
  124.7 24.5 all-reduce.9

commit v2 on v1

v2 whole, which is shorter than its diff:
```python
import functools
import math

import jax
import jax.numpy as jnp
import numpy as np
from jax import lax
from jax.experimental import pallas as pl
from jax.experimental.pallas import tpu as pltpu
from jax.sharding import PartitionSpec as P

HEAD = 64
EPSILON = 1e-05
MASKED = -1000000000.0
LANES = 128
MESH = pl.DeviceIdType.MESH
W = 8
R = 64
LF = 2


class Comm:
    def __init__(self, n, counts, G, O, RF, RU, RD, RL, sems):
        self.nz = n // 4
        self.counts = counts
        self.G, self.O, self.RF, self.RU, self.RD, self.RL = G, O, RF, RU, RD, RL
        self.sems = sems
        d = lax.axis_index("dp")
        self.t = lax.axis_index("tensor")
        self.d = d
        self.z = d // 4
        self.y = (d // 2) % 2
        self.x = d % 2
        self.px = d + 1 - 2 * self.x
        self.py = d + 2 - 4 * self.y

    def steps(self):
        return max(self.counts) + LF + 2 * self.nz + 3

    def barrier(self):
        b = pltpu.get_barrier_semaphore()
        for peer in ((self.px, self.t), (self.py, self.t), (self.d, 1 - self.t)):
            pl.semaphore_signal(b, inc=1, device_id=peer, device_id_type=MESH)

        @pl.when(self.z > 0)
        def _():
            pl.semaphore_signal(b, inc=1, device_id=(self.d - 4, self.t), device_id_type=MESH)

        @pl.when(self.z < self.nz - 1)
        def _():
            pl.semaphore_signal(b, inc=1, device_id=(self.d + 4, self.t), device_id_type=MESH)

        edge = (self.z > 0).astype(jnp.int32) + (self.z < self.nz - 1).astype(jnp.int32)
        pl.semaphore_wait(b, 3 + edge)

    def rows(self, start, size):
        return self.G.at[pl.ds(pl.multiple_of(start, 8), size), :]

    def done(self, start, size):
        return self.O.at[pl.ds(pl.multiple_of(start, 8), size), :]

    def copy(self, src, dst, kind, idx, dev):
        return pltpu.make_async_remote_copy(
            src_ref=src, dst_ref=dst, send_sem=self.sems[kind + "s"].at[idx], recv_sem=self.sems[kind + "r"].at[idx],
            device_id=(dev, self.t), device_id_type=MESH)

    def add(self, start, size, buf):
        r = self.rows(start, size)
        r[...] = r[...] + buf[...]

    def step(self, i):
        for c in (0, 1):
            self.first(c, i)
        for c in (0, 1):
            self.rest(c, i)

    def base(self, c, k):
        return (2 * k + c) * R

    def f_copy(self, c, k):
        a, dev = (self.x, self.px) if c == 0 else (self.y, self.py)
        q = k % W
        return self.copy(self.rows(self.base(c, k) + (1 - a) * (R // 2), R // 2), self.RF.at[c, q], "F", (c, q), dev)

    def first(self, c, i):
        @pl.when(i < self.counts[c])
        def _():
            self.f_copy(c, i).start()

    def rest(self, c, i):
        nz, z = self.nz, self.z
        a, fdev, b, ldev = (self.x, self.px, self.y, self.py) if c == 0 else (self.y, self.py, self.x, self.px)
        n = self.counts[c]
        H, Q, E = R // 2, R // 4, R // 8

        def ok(k):
            return (k >= 0) & (k < n)

        def half(k):
            return self.base(c, k) + a * H

        def sub(k, s):
            return half(k) + s * Q

        def root(k, s):
            return k % 2 if s == 0 else nz - 1 - k % 2

        k = i - LF

        @pl.when(ok(k))
        def _(k=k):
            cp = self.f_copy(c, k)
            cp.wait_send()
            cp.wait_recv()
            self.add(half(k), H, self.RF.at[c, k % W])

        def up(k, s):
            return self.copy(self.rows(sub(k, s), Q), self.RU.at[c, s, k % W], "U", (c, s, k % W), jnp.minimum(self.d + 4, 4 * nz - 1))

        def dn(k, s):
            return self.copy(self.rows(sub(k, s), Q), self.RD.at[c, s, k % W], "D", (c, s, k % W), jnp.maximum(self.d - 4, 0))

        for s in (0, 1):
            k = i - (LF + z)

            @pl.when(ok(k) & (z <= root(k, s)) & (z > 0))
            def _(k=k, s=s):
                up(k, s).wait_recv()
                self.add(sub(k, s), Q, self.RU.at[c, s, k % W])

            @pl.when(ok(k) & (z < root(k, s)))
            def _(k=k, s=s):
                up(k, s).start()

            k = i - (LF + nz - 1 - z)

            @pl.when(ok(k) & (z >= root(k, s)) & (z < nz - 1))
            def _(k=k, s=s):
                dn(k, s).wait_recv()
                self.add(sub(k, s), Q, self.RD.at[c, s, k % W])

            @pl.when(ok(k) & (z > root(k, s)))
            def _(k=k, s=s):
                dn(k, s).start()

            k = i - (LF + z + 1)

            @pl.when(ok(k) & (z < root(k, s)))
            def _(k=k, s=s):
                up(k, s).wait_send()

            k = i - (LF + nz - 1 - z + 1)

            @pl.when(ok(k) & (z > root(k, s)))
            def _(k=k, s=s):
                dn(k, s).wait_send()

        def last(k, s):
            return self.copy(self.rows(sub(k, s) + (1 - b) * E, E), self.RL.at[c, k % W], "L", (c, k % W), ldev)

        def last_back(k, s):
            at = sub(k, s) + b * E
            return self.copy(self.rows(at, E), self.done(at, E), "M", (c, k % W), ldev)

        for s in (0, 1):
            k = i - (LF + nz - 1)

            @pl.when(ok(k) & (z == root(k, s)))
            def _(k=k, s=s):
                last(k, s).start()

            k = i - (LF + nz)

            @pl.when(ok(k) & (z == root(k, s)))
            def _(k=k, s=s):
                cp = last(k, s)
                cp.wait_send()
                cp.wait_recv()
                self.add(sub(k, s) + b * E, E, self.RL.at[c, k % W])
                last_back(k, s).start()
                self.done(sub(k, s) + b * E, E)[...] = self.rows(sub(k, s) + b * E, E)[...]

        def g_up(k, s):
            r = self.done(sub(k, s), Q)
            return self.copy(r, r, "V", (c, s, k % W), jnp.minimum(self.d + 4, 4 * nz - 1))

        def g_dn(k, s):
            r = self.done(sub(k, s), Q)
            return self.copy(r, r, "E", (c, s, k % W), jnp.maximum(self.d - 4, 0))

        def g_first(k, s):
            r = self.done(sub(k, s), Q)
            return self.copy(r, r, "G", (c, s, k % W), fdev)

        for e in (0, 1):
            for s in (0, 1):
                r = e if s == 0 else nz - 1 - e
                lag = LF + nz + 1 + jnp.abs(z - r)
                k = i - lag
                here = ok(k) & (k % 2 == e)

                @pl.when(here & (z == r))
                def _(k=k, s=s):
                    cp = last_back(k, s)
                    cp.wait_send()
                    cp.wait_recv()

                @pl.when(here & (z < r))
                def _(k=k, s=s):
                    g_dn(k, s).wait_recv()

                @pl.when(here & (z > r))
                def _(k=k, s=s):
                    g_up(k, s).wait_recv()

                @pl.when(here & (z <= r) & (z > 0))
                def _(k=k, s=s):
                    g_dn(k, s).start()

                @pl.when(here & (z >= r) & (z < nz - 1))
                def _(k=k, s=s):
                    g_up(k, s).start()

                @pl.when(here)
                def _(k=k, s=s):
                    g_first(k, s).start()

                k = i - (lag + 1)
                here = ok(k) & (k % 2 == e)

                @pl.when(here)
                def _(k=k, s=s):
                    cp = g_first(k, s)
                    cp.wait_send()
                    cp.wait_recv()

                @pl.when(here & (z <= r) & (z > 0))
                def _(k=k, s=s):
                    g_dn(k, s).wait_send()

                @pl.when(here & (z >= r) & (z < nz - 1))
                def _(k=k, s=s):
                    g_up(k, s).wait_send()


KINDS = {"F": (2, W), "U": (2, 2, W), "D": (2, 2, W), "L": (2, W), "M": (2, W), "V": (2, 2, W), "E": (2, 2, W), "G": (2, 2, W)}
SEMS = [k + e for k in KINDS for e in "sr"]


def comm_scratch(width):
    return [
        pltpu.VMEM((2, W, R // 2, width), jnp.float32),
        pltpu.VMEM((2, 2, W, R // 4, width), jnp.float32),
        pltpu.VMEM((2, 2, W, R // 4, width), jnp.float32),
        pltpu.VMEM((2, W, R // 8, width), jnp.float32),
    ] + [pltpu.SemaphoreType.DMA(KINDS[k[0]]) for k in SEMS]

def f32dot(a, b, dims=((1,), (0,))):
    return lax.dot_general(a, b, (dims, ((), ())), preferred_element_type=jnp.float32)


NT = ((1,), (1,))
TN = ((0,), (0,))


def tables(tokens):
    half = HEAD // 2
    frequency = np.exp(np.arange(half) * (-2.0 * math.log(10000.0) / HEAD)).astype(np.float32)
    angles = (np.arange(tokens, dtype=np.float32)[:, None] * frequency[None, :]).astype(np.float64)
    cosine = np.tile(np.cos(angles), (1, LANES // half)).astype(np.float32)
    sign = np.where((np.arange(LANES) // half) % 2 == 0, -1.0, 1.0)
    sine = (np.tile(np.sin(angles), (1, LANES // half)) * sign).astype(np.float32)
    return cosine, sine


def swap_halves(v, low):
    return jnp.where(low, pltpu.roll(v, LANES - HEAD // 2, 1), pltpu.roll(v, HEAD // 2, 1))


def chunks(total, size, body, unroll=False):
    count = total // size

    def one(i, carry):
        body(pl.multiple_of(i * size, size))
        return carry

    lax.fori_loop(0, count, one, 0, unroll=unroll)


def mean_of(v):
    return jnp.mean(v, axis=-1, keepdims=True)


def norm(v):
    centred = v - mean_of(v)
    inv = lax.rsqrt(mean_of(centred * centred) + EPSILON)
    return centred * inv, inv


class Row:
    def __init__(self, ref):
        self.ref = ref

    def __getitem__(self, index):
        v = self.ref[...] if index is Ellipsis else self.ref[index[1]]
        return v.reshape(1, v.shape[0])


def layer_kernel(n, *refs):
    (x_h, ids, ag_h, as_h, wp_h, pb_h, wo_h, ob_h, fg_h, fs_h, we_h, eb_h, ws_h, sb_h, go_h, cos_h, sin_h) = refs[:17]
    O, bo, gi = refs[17:20]
    (x, ag, ash, wp, pb, wo, ob, fg, fs, we, eb, ws, sb, go, cos, sin) = refs[20:36]
    ag, ash, ob, fg, fs, eb, sb = (Row(v) for v in (ag, ash, ob, fg, fs, eb, sb))
    (ain, qkv, att, prob, mid, ein, act, PX, RX, dqkv, G, RF, RU, RD, RL, local, xs, xr) = refs[36:54]
    sems = dict(zip(SEMS, refs[54:]))
    T, D = x.shape
    WL = wo.shape[0]
    FL = ws.shape[0]
    half = T // 2
    parts = WL // LANES
    base_out, base_pack = FL + D * (FL // D), FL + D * (FL // D) + WL
    base_small = base_pack + D + WL
    full = base_small // (2 * R)
    comm = Comm(n, (full + 1, full), G, O, RF, RU, RD, RL, sems)

    loads = []
    for j, (src, dst) in enumerate(
        [(x_h, x), (wp_h, wp), (cos_h, cos), (sin_h, sin), (ag_h, ag.ref), (as_h, ash.ref), (pb_h, pb), (wo_h, wo), (ob_h, ob.ref), (fg_h, fg.ref), (fs_h, fs.ref), (we_h, we), (eb_h, eb.ref), (go_h, go), (ws_h, ws), (sb_h, sb.ref)]
    ):
        cp = pltpu.make_async_copy(src, dst, local.at[j])
        cp.start()
        loads.append(cp)
    comm.barrier()
    for j in (0, 4, 5):
        loads[j].wait()

    lane = lax.broadcasted_iota(jnp.int32, (1, LANES), 1)
    low_half = (lane // (HEAD // 2)) % 2 == 0
    first_head = lane < HEAD
    other = (ids[T - 1] > 0).astype(jnp.float32)
    col = lax.broadcasted_iota(jnp.int32, (1, T), 1)
    top_bias = jnp.where(col < half, 0.0, MASKED * other)
    low_bias = jnp.where(col < half, MASKED * other, 0.0)

    for j in (2, 3):
        loads[j].wait()
    for table in (cos, sin):
        table[pl.ds(half, half), :] = table[pl.ds(half, half), :] * (1.0 - other) + table[pl.ds(0, half), :] * other

    def pre_part(p):
        return G.at[pl.ds(base_pack + p * T, T), :]

    def norm_in(r):
        rows = pl.ds(r, 64)
        normed, _ = norm(x[rows, :].astype(jnp.float32))
        ain[rows, :] = (normed * ag[...] + ash[...]).astype(jnp.bfloat16)

    chunks(T, 64, norm_in)
    for j in (1, 6):
        loads[j].wait()
    tmp = PX.at[0]
    for c in range(3):
        tmp[:, pl.ds(0, WL)] = f32dot(ain[...], wp[c])

        def turn(r, c=c):
            rows = pl.ds(r, 64)
            for j in range(parts):
                v = tmp[rows, pl.ds(j * LANES, LANES)] + pb[pl.ds(c, 1), pl.ds(j * LANES, LANES)]
                if c < 2:
                    v = v * cos[rows, :] + swap_halves(v, low_half) * sin[rows, :]
                if c == 0:
                    v = v.astype(jnp.bfloat16) * jnp.bfloat16(HEAD**-0.5)
                qkv[c * parts + j, rows, :] = v.astype(jnp.bfloat16)

        chunks(T, 64, turn)

    QR = 128

    def attend(j, carry):
        keys, vals = qkv[parts + j], qkv[2 * parts + j]
        for r in range(0, T, QR):
            q = qkv[j, r : r + QR, :]
            bias = top_bias if r < half else low_bias
            outs = []
            for e in (0, 1):
                qm = jnp.where(first_head if e == 0 else ~first_head, q, jnp.zeros_like(q))
                s = f32dot(qm, keys, NT) + bias
                p = jnp.exp(s - jnp.max(s, axis=-1, keepdims=True))
                p = (p * (1.0 / jnp.sum(p, axis=-1, keepdims=True))).astype(jnp.bfloat16)
                prob[2 * j + e, r : r + QR, :] = p
                outs.append(f32dot(p, vals))
            att[r : r + QR, pl.ds(pl.multiple_of(j * LANES, LANES), LANES)] = jnp.where(first_head, *outs).astype(jnp.bfloat16)
        return carry

    lax.fori_loop(0, parts, attend, 0)

    def swap(i, h):
        rows = pl.ds(h * half, half)
        return pltpu.make_async_remote_copy(
            src_ref=PX.at[i % 2, rows, :], dst_ref=RX.at[i % 2, rows, :], send_sem=xs.at[i, h], recv_sem=xr.at[i, h],
            device_id=(comm.d, 1 - comm.t), device_id_type=MESH)

    for j in (7, 8, 9, 10):
        loads[j].wait()
    for h in (0, 1):
        rows = pl.ds(h * half, half)
        PX[0, rows, :] = f32dot(att[rows, :], wo[...])
        swap(0, h).start()
    for h in (0, 1):
        swap(0, h).wait_recv()

        def middle_rows(r, h=h):
            rows = pl.ds(h * half + r, 64)
            v = x[rows, :].astype(jnp.float32) + (PX[0, rows, :] + RX[0, rows, :]) + ob[...]
            mid[rows, :] = v
            normed, _ = norm(v)
            ein[rows, :] = (normed * fg[...] + fs[...]).astype(jnp.bfloat16)

        chunks(half, 64, middle_rows)
    for j in (11, 12):
        loads[j].wait()

    NB = WL
    per = D // NB

    for b in range(FL // NB):
        cols = pl.ds(b * NB, NB)
        here = pl.ds((b % per) * NB, NB)
        pre = pre_part(b // per)
        pre[:, here] = f32dot(ein[...], we[:, cols])

        def gelu_rows(r, pre=pre, here=here, cols=cols):
            rows = pl.ds(r, 64)
            v = pre[rows, here] + eb[:, cols]
            pre[rows, here] = v
            act[rows, cols] = (v * (0.5 + 0.5 * lax.erf(v * math.sqrt(0.5)))).astype(jnp.bfloat16)

        chunks(T, 64, gelu_rows)
    loads[13].wait()
    for b in range(FL // NB):
        G[pl.ds(b * NB, NB), :] = f32dot(act[:, pl.ds(b * NB, NB)], go[...], TN)
    swap(0, 0).wait_send()
    swap(0, 1).wait_send()
    for j in (14, 15):
        loads[j].wait()

    for h in (0, 1):
        rows = pl.ds(h * half, half)
        PX[1, rows, :] = f32dot(act[rows, :], ws[...])
        swap(1, h).start()
    for h in (0, 1):
        swap(1, h).wait()

        def out_rows(r, h=h):
            rows = pl.ds(h * half + r, 64)
            bo[rows, :] = (mid[rows, :] + (PX[1, rows, :] + RX[1, rows, :]) + sb[...]).astype(jnp.bfloat16)

        chunks(half, 64, out_rows)

    def small_row(k):
        return G.at[pl.ds(base_small + k, 1), :]

    for b in range(FL // NB):
        cols = pl.ds(b * NB, NB)
        here = pl.ds((b % per) * NB, NB)
        pre = pre_part(b // per)
        PX[0, :, pl.ds(0, NB)] = f32dot(go[...], ws[cols, :], NT)

        def slope_rows(i, total, pre=pre, here=here, cols=cols):
            rows = pl.ds(pl.multiple_of(i * 64, 64), 64)
            v = pre[rows, here]
            slope = 0.5 + 0.5 * lax.erf(v * math.sqrt(0.5)) + v * (jnp.exp(v * v * -0.5) * (1.0 / math.sqrt(2.0 * math.pi)))
            g = (PX[0, rows, pl.ds(0, NB)] * slope).astype(jnp.bfloat16)
            act[rows, cols] = g
            return total + jnp.sum(g.astype(jnp.float32), axis=0, keepdims=True)

        total = lax.fori_loop(0, T // 64, slope_rows, jnp.zeros((1, NB), jnp.float32))
        G[pl.ds(base_small + 6 + b // per, 1), here] = total
    for p in range(FL // D):
        for b in range(D // NB):
            G[pl.ds(FL + p * D + b * NB, NB), :] = f32dot(ein[:, pl.ds(b * NB, NB)], act[:, pl.ds(p * D, D)], TN)

    for h in (0, 1):
        rows = pl.ds(h * half, half)
        PX[0, rows, :] = f32dot(act[rows, :], we[...], NT)
        swap(2, h).start()

    zero = jnp.zeros((1, D), jnp.float32)
    sums = (zero, zero, zero, zero)
    for h in (0, 1):
        swap(2, h).wait()

        def back_rows(i, totals, h=h):
            rows = pl.ds(pl.multiple_of(h * half + i * 32, 32), 32)
            gain_sum, shift_sum, bias_sum, top_sum = totals
            g = PX[0, rows, :] + RX[0, rows, :]
            normed, inv = norm(mid[rows, :])
            scaled = g * fg[...]
            top = go[rows, :].astype(jnp.float32)
            gm = top + (scaled - mean_of(scaled) - normed * mean_of(scaled * normed)) * inv
            mid[rows, :] = gm
            ein[rows, :] = gm.astype(jnp.bfloat16)
            return (
                gain_sum + jnp.sum(g * normed, axis=0, keepdims=True),
                shift_sum + jnp.sum(g, axis=0, keepdims=True),
                bias_sum + jnp.sum(gm, axis=0, keepdims=True),
                top_sum + jnp.sum(top, axis=0, keepdims=True),
            )

        sums = lax.fori_loop(0, half // 32, back_rows, sums)
    for k, v in zip((3, 4, 2, 5), sums):
        small_row(k)[...] = v

    G[pl.ds(base_out, WL), :] = f32dot(att[...], ein[...], TN)
    att[...] = f32dot(ein[...], wo[...], NT).astype(jnp.bfloat16)

    def attend_back(j, carry):
        keys, vals, queries = qkv[parts + j], qkv[2 * parts + j], qkv[j]
        at = pl.ds(pl.multiple_of(j * LANES, LANES), LANES)
        dv = [None, None]
        dk = [None, None]
        for r in range(0, T, QR):
            rows = pl.ds(r, QR)
            do = att[rows, at]
            q = qkv[j, rows, :]
            dq = []
            for e in (0, 1):
                dom = jnp.where(first_head if e == 0 else ~first_head, do, jnp.zeros_like(do))
                p_low = prob[2 * j + e, rows, :]
                p = p_low.astype(jnp.float32)
                dp = f32dot(dom, vals, NT)
                inner = jnp.sum(p * dp, axis=-1, keepdims=True)
                ds = (p * (dp - inner)).astype(jnp.bfloat16)
                dq.append(f32dot(ds, keys))
                add_v = f32dot(p_low, do, TN)
                add_k = f32dot(ds, q, TN)
                dv[e] = add_v if r == 0 else dv[e] + add_v
                dk[e] = add_k if r == 0 else dk[e] + add_k
            v = jnp.where(first_head, *dq) * (HEAD**-0.5)
            dqkv[j, rows, :] = (v * cos[rows, :] - swap_halves(v, low_half) * sin[rows, :]).astype(jnp.bfloat16)
        dqkv[2 * parts + j] = jnp.where(first_head, *dv).astype(jnp.bfloat16)
        v = jnp.where(first_head, *dk)
        dqkv[parts + j] = (v * cos[...] - swap_halves(v, low_half) * sin[...]).astype(jnp.bfloat16)
        return carry

    lax.fori_loop(0, parts, attend_back, 0)

    for c in range(3):
        for j in range(parts):
            g = dqkv[c * parts + j]
            cols = pl.ds(j * LANES, LANES)
            G[pl.ds(base_small + 8 + c, 1), cols] = jnp.sum(g.astype(jnp.float32), axis=0, keepdims=True)
            grad = f32dot(ain[...], g, TN)
            if c < 2:
                G[pl.ds(base_pack, D), pl.ds(c * WL + j * LANES, LANES)] = grad
            else:
                for p in range(2):
                    G[pl.ds(base_pack + D, WL), pl.ds(p * WL + j * LANES, LANES)] = grad[p * WL : (p + 1) * WL, :]

    for h in (0, 1):
        rows = pl.ds(h * half, half)
        acc = None
        for c in range(3):
            for j in range(parts):
                term = f32dot(dqkv[c * parts + j, rows, :], wp[c, :, pl.ds(j * LANES, LANES)], NT)
                acc = term if acc is None else acc + term
        PX[1, rows, :] = acc
        swap(3, h).start()
    sums = (zero, zero)
    for h in (0, 1):
        swap(3, h).wait()

        def input_rows(i, totals, h=h):
            rows = pl.ds(pl.multiple_of(h * half + i * 32, 32), 32)
            g = PX[1, rows, :] + RX[1, rows, :]
            normed, inv = norm(x[rows, :].astype(jnp.float32))
            scaled = g * ag[...]
            v = mid[rows, :] + (scaled - mean_of(scaled) - normed * mean_of(scaled * normed)) * inv
            gi[rows, :] = v.astype(jnp.bfloat16)
            return (
                totals[0] + jnp.sum(g * normed, axis=0, keepdims=True),
                totals[1] + jnp.sum(g, axis=0, keepdims=True),
            )

        sums = lax.fori_loop(0, half // 32, input_rows, sums)
    small_row(0)[...] = sums[0]
    small_row(1)[...] = sums[1]
    G[pl.ds(base_small + 8, 3), pl.ds(WL, D - WL)] = jnp.zeros((3, D - WL), jnp.float32)
    G[pl.ds(base_small + 11, R - 11), :] = jnp.zeros((R - 11, D), jnp.float32)

    def body(i, carry):
        comm.step(i)
        return carry

    lax.fori_loop(0, comm.steps(), body, 0)


def unpack(moves_of, whole_ref, bo_ref, gi_ref, *refs):
    outs, local = refs[:-1], refs[-1]
    stores = []
    pairs, rows = moves_of(whole_ref, bo_ref, gi_ref, outs)
    for pair in pairs:
        cp = pltpu.make_async_copy(*pair, local.at[len(stores)])
        cp.start()
        stores.append(cp)
    for src, dst in rows:
        dst[...] = src[...]
    for cp in stores:
        cp.wait()


def unpack_moves(T, D, WL, FL, O, bo, gi, outs):
    base_out = FL + D * (FL // D)
    base_pack = base_out + WL
    base_small = base_pack + D + WL
    pairs = [(bo, outs[0]), (gi, outs[1]), (O.at[pl.ds(0, FL), :], outs[2])]
    for p in range(FL // D):
        pairs.append((O.at[pl.ds(FL + p * D, D), :], outs[3].at[:, pl.ds(p * D, D)]))
    pairs.append((O.at[pl.ds(base_out, WL), :], outs[4]))
    for c in range(2):
        pairs.append((O.at[pl.ds(base_pack, D), pl.ds(c * WL, WL)], outs[5].at[c]))
    for p in range(2):
        pairs.append((O.at[pl.ds(base_pack + D, WL), pl.ds(p * WL, WL)], outs[5].at[2, pl.ds(p * WL, WL), :]))
    rows = [(O.at[base_small + k, :], outs[6 + k]) for k in range(6)]
    for p in range(FL // D):
        rows.append((O.at[base_small + 6 + p, :], outs[12].at[pl.ds(p * D, D)]))
    rows.append((O.at[pl.ds(base_small + 8, 3), pl.ds(0, WL)], outs[13]))
    return pairs, rows


def body(
    n_dp,
    block_input,
    sequence_ids,
    attention_gain,
    attention_shift,
    packed_weight,
    packed_bias,
    output_weight,
    output_bias,
    feedforward_gain,
    feedforward_shift,
    expand_weight,
    expand_bias,
    shrink_weight,
    shrink_bias,
    grad_output,
):
    T, D = block_input.shape
    WL = packed_weight.shape[2]
    FL = shrink_weight.shape[0]
    parts = WL // LANES
    bf16, f32 = jnp.bfloat16, jnp.float32
    cosine, sine = tables(T)
    total = FL + D * (FL // D) + WL + D + WL + R

    args = [
        block_input,
        sequence_ids,
        attention_gain,
        attention_shift,
        jnp.transpose(packed_weight, (1, 0, 2)),
        packed_bias,
        output_weight,
        output_bias,
        feedforward_gain,
        feedforward_shift,
        expand_weight,
        expand_bias,
        shrink_weight,
        shrink_bias,
        grad_output,
        jnp.asarray(cosine),
        jnp.asarray(sine),
    ]
    hbm = pl.BlockSpec(memory_space=pltpu.HBM)
    vmem = pl.BlockSpec(memory_space=pltpu.VMEM)
    held = [pltpu.VMEM(a.shape, a.dtype) for i, a in enumerate(args) if i != 1]
    scratch = comm_scratch(D)
    whole, out, grad_in = pl.pallas_call(
        functools.partial(layer_kernel, n_dp),
        out_shape=[pltpu.VMEM((total, D), f32), pltpu.VMEM((T, D), bf16), pltpu.VMEM((T, D), bf16)],
        in_specs=[hbm, pl.BlockSpec(memory_space=pltpu.SMEM)] + [hbm] * 15,
        out_specs=[vmem] * 3,
        scratch_shapes=held
        + [
            pltpu.VMEM((T, D), bf16),
            pltpu.VMEM((3 * parts, T, LANES), bf16),
            pltpu.VMEM((T, WL), bf16),
            pltpu.VMEM((2 * parts, T, T), bf16),
            pltpu.VMEM((T, D), f32),
            pltpu.VMEM((T, D), bf16),
            pltpu.VMEM((T, FL), bf16),
            pltpu.VMEM((2, T, D), f32),
            pltpu.VMEM((2, T, D), f32),
            pltpu.VMEM((3 * parts, T, LANES), bf16),
            pltpu.VMEM((total, D), f32),
        ]
        + scratch[:4]
        + [pltpu.SemaphoreType.DMA((16,)), pltpu.SemaphoreType.DMA((4, 2)), pltpu.SemaphoreType.DMA((4, 2))]
        + scratch[4:],
        compiler_params=pltpu.CompilerParams(
            collective_id=0, has_side_effects=True, vmem_limit_bytes=48 << 20
        ),
    )(*args)
    shapes = [
        ((T, D), bf16),
        ((T, D), bf16),
        ((FL, D), f32),
        ((D, FL), f32),
        ((WL, D), f32),
        ((3, D, WL), f32),
        *[((D,), f32)] * 6,
        ((FL,), f32),
        ((3, WL), f32),
    ]
    anywhere = pl.BlockSpec(memory_space=pl.ANY)
    got = pl.pallas_call(
        functools.partial(unpack, functools.partial(unpack_moves, T, D, WL, FL)),
        out_shape=[pltpu.HBM(*s) for s in shapes[:6]] + [jax.ShapeDtypeStruct(*s) for s in shapes[6:]],
        in_specs=[vmem] * 3,
        out_specs=[anywhere] * 6 + [vmem] * 8,
        scratch_shapes=[pltpu.SemaphoreType.DMA((32,))],
        compiler_params=pltpu.CompilerParams(vmem_limit_bytes=1 << 20),
    )(whole, out, grad_in)
    small = got[6:12]
    return (
        got[0],
        got[1],
        small[0],
        small[1],
        jnp.transpose(got[5], (1, 0, 2)),
        got[13],
        got[4],
        small[2],
        small[3],
        small[4],
        got[3],
        got[12],
        got[2],
        small[5],
    )


def solution(mesh):
    in_specs = (
        P("dp", None),
        P("dp"),
        P(),
        P(),
        P(None, None, "tensor"),
        P(None, "tensor"),
        P("tensor", None),
        P(),
        P(),
        P(),
        P(None, "tensor"),
        P("tensor"),
        P("tensor", None),
        P(),
        P("dp", None),
    )
    out_specs = (
        P("dp", None),
        P("dp", None),
        P(),
        P(),
        P(None, None, "tensor"),
        P(None, "tensor"),
        P("tensor", None),
        P(),
        P(),
        P(),
        P(None, "tensor"),
        P("tensor"),
        P("tensor", None),
        P(),
    )
    return jax.shard_map(
        functools.partial(body, mesh.shape["dp"]), mesh=mesh, in_specs=in_specs, out_specs=out_specs, check_vma=False
    )
```

time: 389 us -> 278 us (0.71)
  Pallas kernels: 212 us -> 277 us
  matrix products: 58 us -> 0 us
  waiting for transfers between devices: 45.5 us -> 0 us
  other arithmetic: 35.2 us -> 0 us
  local copies, waits for them, and re-layouts: 23.1 us -> 0 us
  between operations: 14.5 us -> 0.82 us
    pallas_call x2, Pallas kernels: 212 us -> 277 us  [the longest x1 270 us: body(): pl.pallas_call(functools.partial(layer_kernel, n_dp), out_shape=[pltpu.VM...]
    dot_general x18 -> x0, matrix products: 58 us -> none  [the longest x1 10.1 us: body(): lax.dot_general(grad_output, shrink_weight, contract_cols, preferred_elem...]
    psum x3 -> x0, waiting for transfers between devices: 45.4 us -> none  [the longest x1 23.2 us: body(): lax.psum(jnp.dot(attended, output_weight, preferred_element_type=jnp.floa...]
    reduce_sum x10 -> x0, other arithmetic: 15.4 us -> none  [the longest x1 3.29 us: body(): grad_feedforward_gain = jnp.sum(grad_expand_in * normed_b, axis=0)]
    unnamed x115 -> x0, local copies, waits for them, and re-layouts: 15.4 us -> none
    convert_element_type x5 -> x0, other arithmetic: 14.8 us -> none  [the longest x1 4.74 us: body(): grad_scores = (prob_full * (grad_probs - row_inner)).astype(jnp.bfloat16)]
    slice x5 -> x0, local copies, waits for them, and re-layouts: 4.21 us -> none  [body(): parts.append(flat[place:place + size])]
  transfers between devices with their start and end apart: 3 -> 0, of which waited for: 3 -> 0; matrix products, arithmetic and copies ran while one was open for 6% -> 0% of each run, Pallas kernels for 0% -> 0%
where the time goes in v2:
time: 278 us; the launch traced here: 277 us
  Pallas kernels  277 us (100%)
    pallas_call x1, Pallas kernels, body(): pl.pallas_call(functools.partial(layer_kernel, n_dp), out_shape=[pltpu.VM...  270 us
    pallas_call x1, Pallas kernels, body(): pl.pallas_call(functools.partial(unpack, functools.partial(unpack_moves,...  6.46 us

profile of v2, /device:TPU:0, one launch (start us, length us, event | category | flops | bytes accessed | tf_op | source)
XLA Modules:
  0.0 277.4 jit_solution(2185466325807638844)
XLA Ops:
  0.7 270.1 %shard_map.272 = (f32[4672,768]{1,0:T(8,128)S(1)}, bf16[512,768]{1,0:T(8,128)(2,1)S(1)}, bf16[512,768]{1,0:T(8,128)(2,1)S(1)}) custom-call(bf16[512,768]{1,0:T(8,128)(2,1)} %refs_0_.1, s32[512]{0:T(512)} %refs_1_.1, f32[768]{0:T(1024)} %refs_2_.1, f32[768]{0:T(1024)} %refs_3_.1, bf16[3,768,384]{2,1,0:T(8,128)(2,1)} %bitcast.2, f32[3,384]{1,0:T(4,128)} %refs_5_.1, ...), custom_call_target="tpu_custom_call" | custom-call | tf_op jit(solution)/shard_map/pallas_call | solution.py:680
  270.8 6.5 %shard_map.273 = (bf16[512,768]{1,0:T(8,128)(2,1)}, bf16[512,768]{1,0:T(8,128)(2,1)}, f32[1536,768]{1,0:T(8,128)}, f32[768,1536]{1,0:T(8,128)}, f32[384,768]{1,0...) custom-call(f32[4672,768]{1,0:T(8,128)S(1)} %get-tuple-element.31.wh, ...), custom_call_target="tpu_custom_call" | custom-call | tf_op jit(solution)/shard_map/pallas_call | solution.py:718

commit v3 on v2

--- a/solution.py
+++ b/solution.py
@@ -322,6 +322,20 @@
     base_small = base_pack + D + WL
     full = base_small // (2 * R)
     comm = Comm(n, (full + 1, full), G, O, RF, RU, RD, RL, sems)
+    at_step = [0]
+
+    def tick(count=1):
+        if count == 1:
+            comm.step(jnp.int32(at_step[0]))
+        else:
+
+            def one(i, carry):
+                comm.step(i)
+                return carry
+
+            lax.fori_loop(at_step[0], at_step[0] + count, one, 0)
+        at_step[0] += count
+
 
     loads = []
     for j, (src, dst) in enumerate(
@@ -439,6 +453,7 @@
     loads[13].wait()
     for b in range(FL // NB):
         G[pl.ds(b * NB, NB), :] = f32dot(act[:, pl.ds(b * NB, NB)], go[...], TN)
+    tick(2)
     swap(0, 0).wait_send()
     swap(0, 1).wait_send()
     for j in (14, 15):
@@ -448,6 +463,7 @@
         rows = pl.ds(h * half, half)
         PX[1, rows, :] = f32dot(act[rows, :], ws[...])
         swap(1, h).start()
+    tick()
     for h in (0, 1):
         swap(1, h).wait()
 
@@ -456,6 +472,7 @@
             bo[rows, :] = (mid[rows, :] + (PX[1, rows, :] + RX[1, rows, :]) + sb[...]).astype(jnp.bfloat16)
 
         chunks(half, 64, out_rows)
+        tick()
 
     def small_row(k):
         return G.at[pl.ds(base_small + k, 1), :]
@@ -476,14 +493,17 @@
 
         total = lax.fori_loop(0, T // 64, slope_rows, jnp.zeros((1, NB), jnp.float32))
         G[pl.ds(base_small + 6 + b // per, 1), here] = total
+        tick()
     for p in range(FL // D):
         for b in range(D // NB):
             G[pl.ds(FL + p * D + b * NB, NB), :] = f32dot(ein[:, pl.ds(b * NB, NB)], act[:, pl.ds(p * D, D)], TN)
+        tick()
 
     for h in (0, 1):
         rows = pl.ds(h * half, half)
         PX[0, rows, :] = f32dot(act[rows, :], we[...], NT)
         swap(2, h).start()
+    tick()
 
     zero = jnp.zeros((1, D), jnp.float32)
     sums = (zero, zero, zero, zero)
@@ -508,10 +528,12 @@
             )
 
         sums = lax.fori_loop(0, half // 32, back_rows, sums)
+        tick()
     for k, v in zip((3, 4, 2, 5), sums):
         small_row(k)[...] = v
 
     G[pl.ds(base_out, WL), :] = f32dot(att[...], ein[...], TN)
+    tick()
     att[...] = f32dot(ein[...], wo[...], NT).astype(jnp.bfloat16)
 
     def attend_back(j, carry):
@@ -538,12 +560,15 @@
                 dk[e] = add_k if r == 0 else dk[e] + add_k
             v = jnp.where(first_head, *dq) * (HEAD**-0.5)
             dqkv[j, rows, :] = (v * cos[rows, :] - swap_halves(v, low_half) * sin[rows, :]).astype(jnp.bfloat16)
+            if (r // QR) % 2 == 1:
+                comm.step(at_step[0] + 2 * j + r // (2 * QR))
         dqkv[2 * parts + j] = jnp.where(first_head, *dv).astype(jnp.bfloat16)
         v = jnp.where(first_head, *dk)
         dqkv[parts + j] = (v * cos[...] - swap_halves(v, low_half) * sin[...]).astype(jnp.bfloat16)
         return carry
 
     lax.fori_loop(0, parts, attend_back, 0)
+    at_step[0] += 2 * parts
 
     for c in range(3):
         for j in range(parts):
@@ -556,6 +581,7 @@
             else:
                 for p in range(2):
                     G[pl.ds(base_pack + D, WL), pl.ds(p * WL + j * LANES, LANES)] = grad[p * WL : (p + 1) * WL, :]
+        tick()
 
     for h in (0, 1):
         rows = pl.ds(h * half, half)
@@ -566,6 +592,7 @@
                 acc = term if acc is None else acc + term
         PX[1, rows, :] = acc
         swap(3, h).start()
+    tick()
     sums = (zero, zero)
     for h in (0, 1):
         swap(3, h).wait()
@@ -583,16 +610,13 @@
             )
 
         sums = lax.fori_loop(0, half // 32, input_rows, sums)
+        tick()
     small_row(0)[...] = sums[0]
     small_row(1)[...] = sums[1]
     G[pl.ds(base_small + 8, 3), pl.ds(WL, D - WL)] = jnp.zeros((3, D - WL), jnp.float32)
     G[pl.ds(base_small + 11, R - 11), :] = jnp.zeros((R - 11, D), jnp.float32)
 
-    def body(i, carry):
-        comm.step(i)
-        return carry
-
-    lax.fori_loop(0, comm.steps(), body, 0)
+    tick(comm.steps() - at_step[0])
 
 
 def unpack(moves_of, whole_ref, bo_ref, gi_ref, *refs):

time: 278 us -> 241 us (0.87)
  Pallas kernels: 277 us -> 240 us
    pallas_call x1, Pallas kernels: 270 us -> 233 us  [body(): pl.pallas_call(functools.partial(layer_kernel, n_dp), out_shape=[pltpu.VM...]
where the time goes in v3:
time: 241 us
  Pallas kernels  240 us (100%)
    pallas_call x1, Pallas kernels, body(): pl.pallas_call(functools.partial(layer_kernel, n_dp), out_shape=[pltpu.VM...  233 us
    pallas_call x1, Pallas kernels, body(): pl.pallas_call(functools.partial(unpack, functools.partial(unpack_moves,...  6.46 us

profile of v3, /device:TPU:0, one launch (start us, length us, event | category | flops | bytes accessed | tf_op | source)
XLA Modules:
  0.0 240.7 jit_solution(6770879129571511997)
XLA Ops:
  0.7 233.4 %shard_map.272 = (f32[4672,768]{1,0:T(8,128)S(1)}, bf16[512,768]{1,0:T(8,128)(2,1)S(1)}, bf16[512,768]{1,0:T(8,128)(2,1)S(1)}) custom-call(bf16[512,768]{1,0:T(8,128)(2,1)} %refs_0_.1, s32[512]{0:T(512)} %refs_1_.1, f32[768]{0:T(1024)} %refs_2_.1, f32[768]{0:T(1024)} %refs_3_.1, bf16[3,768,384]{2,1,0:T(8,128)(2,1)} %bitcast.2, f32[3,384]{1,0:T(4,128)} %refs_5_.1, ...), custom_call_target="tpu_custom_call" | custom-call | tf_op jit(solution)/shard_map/pallas_call | solution.py:704
  234.1 6.5 %shard_map.273 = (bf16[512,768]{1,0:T(8,128)(2,1)}, bf16[512,768]{1,0:T(8,128)(2,1)}, f32[1536,768]{1,0:T(8,128)}, f32[768,1536]{1,0:T(8,128)}, f32[384,768]{1,0...) custom-call(f32[4672,768]{1,0:T(8,128)S(1)} %get-tuple-element.31.wh, ...), custom_call_target="tpu_custom_call" | custom-call | tf_op jit(solution)/shard_map/pallas_call | solution.py:742

commit v4 on v2

--- a/solution.py
+++ b/solution.py
@@ -37,7 +37,7 @@
     def steps(self):
         return max(self.counts) + LF + 2 * self.nz + 3
 
-    def barrier(self):
+    def arrive(self):
         b = pltpu.get_barrier_semaphore()
         for peer in ((self.px, self.t), (self.py, self.t), (self.d, 1 - self.t)):
             pl.semaphore_signal(b, inc=1, device_id=peer, device_id_type=MESH)
@@ -50,8 +50,9 @@
         def _():
             pl.semaphore_signal(b, inc=1, device_id=(self.d + 4, self.t), device_id_type=MESH)
 
+    def ready(self):
         edge = (self.z > 0).astype(jnp.int32) + (self.z < self.nz - 1).astype(jnp.int32)
-        pl.semaphore_wait(b, 3 + edge)
+        pl.semaphore_wait(pltpu.get_barrier_semaphore(), 3 + edge)
 
     def rows(self, start, size):
         return self.G.at[pl.ds(pl.multiple_of(start, 8), size), :]
@@ -311,8 +312,8 @@
     O, bo, gi = refs[17:20]
     (x, ag, ash, wp, pb, wo, ob, fg, fs, we, eb, ws, sb, go, cos, sin) = refs[20:36]
     ag, ash, ob, fg, fs, eb, sb = (Row(v) for v in (ag, ash, ob, fg, fs, eb, sb))
-    (ain, qkv, att, prob, mid, ein, act, PX, RX, dqkv, G, RF, RU, RD, RL, local, xs, xr) = refs[36:54]
-    sems = dict(zip(SEMS, refs[54:]))
+    (ain, qkv, att, prob, mid, ein, act, PX, RX, dqkv, G, RF, RU, RD, RL, local, xs, xr, ys, yr, bias2) = refs[36:57]
+    sems = dict(zip(SEMS, refs[57:]))
     T, D = x.shape
     WL = wo.shape[0]
     FL = ws.shape[0]
@@ -322,17 +323,31 @@
     base_small = base_pack + D + WL
     full = base_small // (2 * R)
     comm = Comm(n, (full + 1, full), G, O, RF, RU, RD, RL, sems)
+    at_step = [0]
+
+    def tick(more=0):
+        comm.step(jnp.int32(at_step[0]) + more)
+
+    def passed(count):
+        at_step[0] += count
 
     loads = []
     for j, (src, dst) in enumerate(
-        [(x_h, x), (wp_h, wp), (cos_h, cos), (sin_h, sin), (ag_h, ag.ref), (as_h, ash.ref), (pb_h, pb), (wo_h, wo), (ob_h, ob.ref), (fg_h, fg.ref), (fs_h, fs.ref), (we_h, we), (eb_h, eb.ref), (go_h, go), (ws_h, ws), (sb_h, sb.ref)]
+        [(x_h, x), (wp_h.at[0], wp.at[0]), (cos_h, cos), (sin_h, sin), (ag_h, ag.ref), (as_h, ash.ref), (pb_h, pb), (wo_h, wo), (ob_h, ob.ref), (fg_h, fg.ref), (fs_h, fs.ref), (we_h, we), (eb_h, eb.ref), (go_h, go), (ws_h, ws), (sb_h, sb.ref), (wp_h.at[1], wp.at[1]), (wp_h.at[2], wp.at[2])]
     ):
-        cp = pltpu.make_async_copy(src, dst, local.at[j])
-        cp.start()
-        loads.append(cp)
-    comm.barrier()
-    for j in (0, 4, 5):
-        loads[j].wait()
+        loads.append(pltpu.make_async_copy(src, dst, local.at[j]))
+
+    def begin(*which):
+        for j in which:
+            loads[j].start()
+
+    def arrived(*which):
+        for j in which:
+            loads[j].wait()
+
+    begin(0, 4, 5, 1, 2, 3, 6, 16, 17)
+    comm.arrive()
+    arrived(0, 4, 5)
 
     lane = lax.broadcasted_iota(jnp.int32, (1, LANES), 1)
     low_half = (lane // (HEAD // 2)) % 2 == 0
@@ -342,13 +357,8 @@
     top_bias = jnp.where(col < half, 0.0, MASKED * other)
     low_bias = jnp.where(col < half, MASKED * other, 0.0)
 
-    for j in (2, 3):
-        loads[j].wait()
-    for table in (cos, sin):
-        table[pl.ds(half, half), :] = table[pl.ds(half, half), :] * (1.0 - other) + table[pl.ds(0, half), :] * other
-
     def pre_part(p):
-        return G.at[pl.ds(base_pack + p * T, T), :]
+        return G.at[pl.ds(pl.multiple_of(base_pack + p * T, 8), T), :]
 
     def norm_in(r):
         rows = pl.ds(r, 64)
@@ -356,10 +366,14 @@
         ain[rows, :] = (normed * ag[...] + ash[...]).astype(jnp.bfloat16)
 
     chunks(T, 64, norm_in)
-    for j in (1, 6):
-        loads[j].wait()
+    arrived(1, 2, 3, 6)
+    begin(7, 8, 9, 10, 11, 12, 13, 14, 15)
+    for table in (cos, sin):
+        table[pl.ds(half, half), :] = table[pl.ds(half, half), :] * (1.0 - other) + table[pl.ds(0, half), :] * other
     tmp = PX.at[0]
     for c in range(3):
+        if c > 0:
+            arrived(15 + c)
         tmp[:, pl.ds(0, WL)] = f32dot(ain[...], wp[c])
 
         def turn(r, c=c):
@@ -375,98 +389,120 @@
         chunks(T, 64, turn)
 
     QR = 128
-
-    def attend(j, carry):
-        keys, vals = qkv[parts + j], qkv[2 * parts + j]
-        for r in range(0, T, QR):
-            q = qkv[j, r : r + QR, :]
-            bias = top_bias if r < half else low_bias
-            outs = []
-            for e in (0, 1):
-                qm = jnp.where(first_head if e == 0 else ~first_head, q, jnp.zeros_like(q))
-                s = f32dot(qm, keys, NT) + bias
-                p = jnp.exp(s - jnp.max(s, axis=-1, keepdims=True))
-                p = (p * (1.0 / jnp.sum(p, axis=-1, keepdims=True))).astype(jnp.bfloat16)
-                prob[2 * j + e, r : r + QR, :] = p
-                outs.append(f32dot(p, vals))
-            att[r : r + QR, pl.ds(pl.multiple_of(j * LANES, LANES), LANES)] = jnp.where(first_head, *outs).astype(jnp.bfloat16)
-        return carry
-
-    lax.fori_loop(0, parts, attend, 0)
+    blocks = T // QR
+
+    def first_swap(i):
+        rows = pl.ds(pl.multiple_of(i * QR, QR), QR)
+        return pltpu.make_async_remote_copy(
+            src_ref=PX.at[0, rows, :], dst_ref=RX.at[0, rows, :], send_sem=ys.at[i], recv_sem=yr.at[i],
+            device_id=(comm.d, 1 - comm.t), device_id_type=MESH)
 
     def swap(i, h):
-        rows = pl.ds(h * half, half)
+        rows = pl.ds(pl.multiple_of(h * half, half), half)
         return pltpu.make_async_remote_copy(
             src_ref=PX.at[i % 2, rows, :], dst_ref=RX.at[i % 2, rows, :], send_sem=xs.at[i, h], recv_sem=xr.at[i, h],
             device_id=(comm.d, 1 - comm.t), device_id_type=MESH)
 
-    for j in (7, 8, 9, 10):
-        loads[j].wait()
-    for h in (0, 1):
-        rows = pl.ds(h * half, half)
+    arrived(7, 8, 9, 10)
+    comm.ready()
+
+    def attend(i, carry):
+        rows = pl.ds(pl.multiple_of(i * QR, QR), QR)
+        bias = jnp.where(i < blocks // 2, top_bias, low_bias)
+        for j in range(parts):
+            keys, vals = qkv[parts + j], qkv[2 * parts + j]
+            q = qkv[j, rows, :]
+            zeros = jnp.zeros_like(q)
+            two = jnp.concatenate([jnp.where(first_head, q, zeros), jnp.where(first_head, zeros, q)], axis=0)
+            s = f32dot(two, keys, NT) + bias
+            p = jnp.exp(s - jnp.max(s, axis=-1, keepdims=True))
+            p = (p * (1.0 / jnp.sum(p, axis=-1, keepdims=True))).astype(jnp.bfloat16)
+            prob[2 * j, rows, :] = p[:QR]
+            prob[2 * j + 1, rows, :] = p[QR:]
+            out = f32dot(p, vals)
+            att[rows, j * LANES : (j + 1) * LANES] = jnp.where(first_head, out[:QR], out[QR:]).astype(jnp.bfloat16)
         PX[0, rows, :] = f32dot(att[rows, :], wo[...])
-        swap(0, h).start()
-    for h in (0, 1):
-        swap(0, h).wait_recv()
-
-        def middle_rows(r, h=h):
-            rows = pl.ds(h * half + r, 64)
+        first_swap(i).start()
+        return carry
+
+    lax.fori_loop(0, blocks, attend, 0)
+
+    def middle_block(i, carry):
+        first_swap(i).wait_recv()
+
+        def middle_rows(r):
+            rows = pl.ds(pl.multiple_of(i * QR + r, 64), 64)
             v = x[rows, :].astype(jnp.float32) + (PX[0, rows, :] + RX[0, rows, :]) + ob[...]
             mid[rows, :] = v
             normed, _ = norm(v)
             ein[rows, :] = (normed * fg[...] + fs[...]).astype(jnp.bfloat16)
 
-        chunks(half, 64, middle_rows)
-    for j in (11, 12):
-        loads[j].wait()
+        chunks(QR, 64, middle_rows, True)
+        return carry
+
+    lax.fori_loop(0, blocks, middle_block, 0)
+    arrived(11, 12, 13)
 
     NB = WL
     per = D // NB
 
-    for b in range(FL // NB):
-        cols = pl.ds(b * NB, NB)
-        here = pl.ds((b % per) * NB, NB)
-        pre = pre_part(b // per)
+    nb = FL // NB
+    for b in range(nb):
+        bias2[pl.ds(b, 1), :] = eb[:, pl.ds(b * NB, NB)]
+
+    def places(b):
+        cols = pl.ds(pl.multiple_of(b * NB, LANES), NB)
+        here = pl.ds(pl.multiple_of((b % per) * NB, LANES), NB)
+        return cols, here, pre_part(b // per)
+
+    def expand(b, carry):
+        cols, here, pre = places(b)
         pre[:, here] = f32dot(ein[...], we[:, cols])
 
-        def gelu_rows(r, pre=pre, here=here, cols=cols):
+        def gelu_rows(r):
             rows = pl.ds(r, 64)
-            v = pre[rows, here] + eb[:, cols]
+            v = pre[rows, here] + bias2[pl.ds(b, 1), :]
             pre[rows, here] = v
             act[rows, cols] = (v * (0.5 + 0.5 * lax.erf(v * math.sqrt(0.5)))).astype(jnp.bfloat16)
 
         chunks(T, 64, gelu_rows)
-    loads[13].wait()
-    for b in range(FL // NB):
-        G[pl.ds(b * NB, NB), :] = f32dot(act[:, pl.ds(b * NB, NB)], go[...], TN)
-    swap(0, 0).wait_send()
-    swap(0, 1).wait_send()
-    for j in (14, 15):
-        loads[j].wait()
+        G[pl.ds(pl.multiple_of(b * NB, LANES), NB), :] = f32dot(act[:, cols], go[...], TN)
+        tick(b)
+        return carry
+
+    lax.fori_loop(0, nb, expand, 0)
+    passed(nb)
+    for i in range(blocks):
+        first_swap(i).wait_send()
+    arrived(14, 15)
 
     for h in (0, 1):
         rows = pl.ds(h * half, half)
         PX[1, rows, :] = f32dot(act[rows, :], ws[...])
         swap(1, h).start()
-    for h in (0, 1):
+
+    def out_half(h, carry):
+        tick(h)
         swap(1, h).wait()
 
-        def out_rows(r, h=h):
-            rows = pl.ds(h * half + r, 64)
+        def out_rows(r):
+            rows = pl.ds(pl.multiple_of(h * half + r, 64), 64)
             bo[rows, :] = (mid[rows, :] + (PX[1, rows, :] + RX[1, rows, :]) + sb[...]).astype(jnp.bfloat16)
 
         chunks(half, 64, out_rows)
+        return carry
+
+    lax.fori_loop(0, 2, out_half, 0)
+    passed(2)
 
     def small_row(k):
         return G.at[pl.ds(base_small + k, 1), :]
 
-    for b in range(FL // NB):
-        cols = pl.ds(b * NB, NB)
-        here = pl.ds((b % per) * NB, NB)
-        pre = pre_part(b // per)
+    def slope(b, carry):
+        cols, here, pre = places(b)
         PX[0, :, pl.ds(0, NB)] = f32dot(go[...], ws[cols, :], NT)
 
-        def slope_rows(i, total, pre=pre, here=here, cols=cols):
+        def slope_rows(i, total):
             rows = pl.ds(pl.multiple_of(i * 64, 64), 64)
             v = pre[rows, here]
             slope = 0.5 + 0.5 * lax.erf(v * math.sqrt(0.5)) + v * (jnp.exp(v * v * -0.5) * (1.0 / math.sqrt(2.0 * math.pi)))
@@ -474,23 +510,38 @@
             act[rows, cols] = g
             return total + jnp.sum(g.astype(jnp.float32), axis=0, keepdims=True)
 
-        total = lax.fori_loop(0, T // 64, slope_rows, jnp.zeros((1, NB), jnp.float32))
-        G[pl.ds(base_small + 6 + b // per, 1), here] = total
-    for p in range(FL // D):
-        for b in range(D // NB):
-            G[pl.ds(FL + p * D + b * NB, NB), :] = f32dot(ein[:, pl.ds(b * NB, NB)], act[:, pl.ds(p * D, D)], TN)
+        bias2[pl.ds(b, 1), :] = lax.fori_loop(0, T // 64, slope_rows, jnp.zeros((1, NB), jnp.float32))
+        tick(b)
+        return carry
+
+    lax.fori_loop(0, nb, slope, 0)
+    passed(nb)
+    for b in range(nb):
+        G[pl.ds(base_small + 6 + b // per, 1), pl.ds((b % per) * NB, NB)] = bias2[pl.ds(b, 1), :]
+
+    def expand_grad(b, carry):
+        source = pl.ds(pl.multiple_of((b % per) * NB, LANES), NB)
+        wide = pl.ds(pl.multiple_of((b // per) * D, LANES), D)
+        G[pl.ds(pl.multiple_of(FL + b * NB, LANES), NB), :] = f32dot(ein[:, source], act[:, wide], TN)
+        tick(b)
+        return carry
+
+    lax.fori_loop(0, nb, expand_grad, 0)
+    passed(nb)
 
     for h in (0, 1):
         rows = pl.ds(h * half, half)
         PX[0, rows, :] = f32dot(act[rows, :], we[...], NT)
         swap(2, h).start()
+    tick()
+    passed(1)
 
     zero = jnp.zeros((1, D), jnp.float32)
-    sums = (zero, zero, zero, zero)
-    for h in (0, 1):
+
+    def back_half(h, totals):
         swap(2, h).wait()
 
-        def back_rows(i, totals, h=h):
+        def back_rows(i, totals):
             rows = pl.ds(pl.multiple_of(h * half + i * 32, 32), 32)
             gain_sum, shift_sum, bias_sum, top_sum = totals
             g = PX[0, rows, :] + RX[0, rows, :]
@@ -507,12 +558,19 @@
                 top_sum + jnp.sum(top, axis=0, keepdims=True),
             )
 
-        sums = lax.fori_loop(0, half // 32, back_rows, sums)
+        totals = lax.fori_loop(0, half // 32, back_rows, totals)
+        tick(h)
+        return totals
+
+    sums = lax.fori_loop(0, 2, back_half, (zero, zero, zero, zero))
+    passed(2)
     for k, v in zip((3, 4, 2, 5), sums):
         small_row(k)[...] = v
 
     G[pl.ds(base_out, WL), :] = f32dot(att[...], ein[...], TN)
     att[...] = f32dot(ein[...], wo[...], NT).astype(jnp.bfloat16)
+    tick()
+    passed(1)
 
     def attend_back(j, carry):
         keys, vals, queries = qkv[parts + j], qkv[2 * parts + j], qkv[j]
@@ -538,39 +596,44 @@
                 dk[e] = add_k if r == 0 else dk[e] + add_k
             v = jnp.where(first_head, *dq) * (HEAD**-0.5)
             dqkv[j, rows, :] = (v * cos[rows, :] - swap_halves(v, low_half) * sin[rows, :]).astype(jnp.bfloat16)
+            if (r // QR) % 2 == 1:
+                tick(2 * j + r // (2 * QR))
         dqkv[2 * parts + j] = jnp.where(first_head, *dv).astype(jnp.bfloat16)
         v = jnp.where(first_head, *dk)
         dqkv[parts + j] = (v * cos[...] - swap_halves(v, low_half) * sin[...]).astype(jnp.bfloat16)
         return carry
 
     lax.fori_loop(0, parts, attend_back, 0)
+    passed(2 * parts)
+
+    def joined(c, rows):
+        return jnp.concatenate([dqkv[c * parts + j, rows, :] for j in range(parts)], axis=1)
 
     for c in range(3):
-        for j in range(parts):
-            g = dqkv[c * parts + j]
-            cols = pl.ds(j * LANES, LANES)
-            G[pl.ds(base_small + 8 + c, 1), cols] = jnp.sum(g.astype(jnp.float32), axis=0, keepdims=True)
-            grad = f32dot(ain[...], g, TN)
-            if c < 2:
-                G[pl.ds(base_pack, D), pl.ds(c * WL + j * LANES, LANES)] = grad
-            else:
-                for p in range(2):
-                    G[pl.ds(base_pack + D, WL), pl.ds(p * WL + j * LANES, LANES)] = grad[p * WL : (p + 1) * WL, :]
+        g = joined(c, pl.ds(0, T))
+        G[pl.ds(base_small + 8 + c, 1), pl.ds(0, WL)] = jnp.sum(g.astype(jnp.float32), axis=0, keepdims=True)
+        grad = f32dot(ain[...], g, TN)
+        if c < 2:
+            G[pl.ds(base_pack, D), pl.ds(c * WL, WL)] = grad
+        else:
+            for p in range(2):
+                G[pl.ds(base_pack + D, WL), pl.ds(p * WL, WL)] = grad[p * WL : (p + 1) * WL, :]
+    tick()
+    passed(1)
 
     for h in (0, 1):
         rows = pl.ds(h * half, half)
-        acc = None
-        for c in range(3):
-            for j in range(parts):
-                term = f32dot(dqkv[c * parts + j, rows, :], wp[c, :, pl.ds(j * LANES, LANES)], NT)
-                acc = term if acc is None else acc + term
+        acc = f32dot(joined(0, rows), wp[0], NT)
+        for c in (1, 2):
+            acc = acc + f32dot(joined(c, rows), wp[c], NT)
         PX[1, rows, :] = acc
         swap(3, h).start()
-    sums = (zero, zero)
-    for h in (0, 1):
+
+    def input_half(h, totals):
+        tick(h)
         swap(3, h).wait()
 
-        def input_rows(i, totals, h=h):
+        def input_rows(i, totals):
             rows = pl.ds(pl.multiple_of(h * half + i * 32, 32), 32)
             g = PX[1, rows, :] + RX[1, rows, :]
             normed, inv = norm(x[rows, :].astype(jnp.float32))
@@ -582,7 +645,10 @@
                 totals[1] + jnp.sum(g, axis=0, keepdims=True),
             )
 
-        sums = lax.fori_loop(0, half // 32, input_rows, sums)
+        return lax.fori_loop(0, half // 32, input_rows, totals)
+
+    sums = lax.fori_loop(0, 2, input_half, (zero, zero))
+    passed(2)
     small_row(0)[...] = sums[0]
     small_row(1)[...] = sums[1]
     G[pl.ds(base_small + 8, 3), pl.ds(WL, D - WL)] = jnp.zeros((3, D - WL), jnp.float32)
@@ -592,7 +658,7 @@
         comm.step(i)
         return carry
 
-    lax.fori_loop(0, comm.steps(), body, 0)
+    lax.fori_loop(at_step[0], comm.steps(), body, 0)
 
 
 def unpack(moves_of, whole_ref, bo_ref, gi_ref, *refs):
@@ -697,7 +763,8 @@
             pltpu.VMEM((total, D), f32),
         ]
         + scratch[:4]
-        + [pltpu.SemaphoreType.DMA((16,)), pltpu.SemaphoreType.DMA((4, 2)), pltpu.SemaphoreType.DMA((4, 2))]
+        + [pltpu.SemaphoreType.DMA((18,)), pltpu.SemaphoreType.DMA((4, 2)), pltpu.SemaphoreType.DMA((4, 2))]
+        + [pltpu.SemaphoreType.DMA((T // 128,)), pltpu.SemaphoreType.DMA((T // 128,)), pltpu.VMEM((FL // WL, WL), f32)]
         + scratch[4:],
         compiler_params=pltpu.CompilerParams(
             collective_id=0, has_side_effects=True, vmem_limit_bytes=48 << 20

time: 278 us -> 231 us (0.83)
  Pallas kernels: 277 us -> 230 us
    pallas_call x1, Pallas kernels: 270 us -> 224 us  [body(): pl.pallas_call(functools.partial(layer_kernel, n_dp), out_shape=[pltpu.VM...]
where the time goes in v4:
time: 231 us
  Pallas kernels  230 us (100%)
    pallas_call x1, Pallas kernels, body(): pl.pallas_call(functools.partial(layer_kernel, n_dp), out_shape=[pltpu.VM...  224 us
    pallas_call x1, Pallas kernels, body(): pl.pallas_call(functools.partial(unpack, functools.partial(unpack_moves,...  6.46 us

profile of v4, /device:TPU:0, one launch (start us, length us, event | category | flops | bytes accessed | tf_op | source)
XLA Modules:
  0.0 231.1 jit_solution(14949690422441030890)
XLA Ops:
  0.7 223.8 %shard_map.272 = (f32[4672,768]{1,0:T(8,128)S(1)}, bf16[512,768]{1,0:T(8,128)(2,1)S(1)}, bf16[512,768]{1,0:T(8,128)(2,1)S(1)}) custom-call(bf16[512,768]{1,0:T(8,128)(2,1)} %refs_0_.1, s32[512]{0:T(512)} %refs_1_.1, f32[768]{0:T(1024)} %refs_2_.1, f32[768]{0:T(1024)} %refs_3_.1, bf16[3,768,384]{2,1,0:T(8,128)(2,1)} %bitcast.2, f32[3,384]{1,0:T(4,128)} %refs_5_.1, ...), custom_call_target="tpu_custom_call" | custom-call | tf_op jit(solution)/shard_map/pallas_call | solution.py:746
  224.5 6.5 %shard_map.273 = (bf16[512,768]{1,0:T(8,128)(2,1)}, bf16[512,768]{1,0:T(8,128)(2,1)}, f32[1536,768]{1,0:T(8,128)}, f32[768,1536]{1,0:T(8,128)}, f32[384,768]{1,0...) custom-call(f32[4672,768]{1,0:T(8,128)S(1)} %get-tuple-element.31.wh, ...), custom_call_target="tpu_custom_call" | custom-call | tf_op jit(solution)/shard_map/pallas_call | solution.py:785

commit v5 on v4

--- a/solution.py
+++ b/solution.py
@@ -14,16 +14,21 @@
 MASKED = -1000000000.0
 LANES = 128
 MESH = pl.DeviceIdType.MESH
-W = 8
+W = 4
+WF = 8
 R = 64
 LF = 2
+AHEAD = 1
+SMALL = 16
 
 
 class Comm:
-    def __init__(self, n, counts, G, O, RF, RU, RD, RL, sems):
+    def __init__(self, n, counts, G, O, RF, RU, RD, RL, RS, sems):
         self.nz = n // 4
         self.counts = counts
         self.G, self.O, self.RF, self.RU, self.RD, self.RL = G, O, RF, RU, RD, RL
+        self.RS = RS
+        self.credits = self.nz > W
         self.sems = sems
         d = lax.axis_index("dp")
         self.t = lax.axis_index("tensor")
@@ -35,7 +40,7 @@
         self.py = d + 2 - 4 * self.y
 
     def steps(self):
-        return max(self.counts) + LF + 2 * self.nz + 3
+        return max(self.counts) + LF + 2 * self.nz
 
     def arrive(self):
         b = pltpu.get_barrier_semaphore()
@@ -61,9 +66,20 @@
         return self.O.at[pl.ds(pl.multiple_of(start, 8), size), :]
 
     def copy(self, src, dst, kind, idx, dev):
+        sent, landed = ("U" if kind == "D" else kind) + "s", ("V" if kind == "E" else kind) + "r"
         return pltpu.make_async_remote_copy(
-            src_ref=src, dst_ref=dst, send_sem=self.sems[kind + "s"].at[idx], recv_sem=self.sems[kind + "r"].at[idx],
+            src_ref=src, dst_ref=dst, send_sem=self.sems[sent].at[idx], recv_sem=self.sems[landed].at[idx],
             device_id=(dev, self.t), device_id_type=MESH)
+
+    def give(self, cond, kind, c, s, dev):
+        @pl.when(cond)
+        def _():
+            pl.semaphore_signal(self.sems[kind].at[c, s], inc=1, device_id=(dev, self.t), device_id_type=MESH)
+
+    def take(self, cond, kind, c, s):
+        @pl.when(cond)
+        def _():
+            pl.semaphore_wait(self.sems[kind].at[c, s], 1)
 
     def add(self, start, size, buf):
         r = self.rows(start, size)
@@ -78,21 +94,79 @@
     def base(self, c, k):
         return (2 * k + c) * R
 
+    def small(self, i, at):
+        nz, z = self.nz, self.z
+        src, dst = self.rows(at, SMALL), self.done(at, SMALL)
+        pairs = [self.copy(src, self.RS.at[j], "S", (j,), dev) for j, dev in ((0, self.px), (1, self.py))]
+        up = self.copy(src, self.RS.at[2], "S", (2,), jnp.minimum(self.d + 4, 4 * nz - 1))
+        down = self.copy(dst, dst, "S", (3,), jnp.maximum(self.d - 4, 0))
+
+        @pl.when(i == 0)
+        def _():
+            pairs[0].start()
+
+        @pl.when(i == 1)
+        def _():
+            pairs[0].wait()
+            self.add(at, SMALL, self.RS.at[0])
+            pairs[1].start()
+
+        @pl.when(i == 2)
+        def _():
+            pairs[1].wait()
+            self.add(at, SMALL, self.RS.at[1])
+
+        @pl.when((i == 2 + z) & (z > 0))
+        def _():
+            up.wait_recv()
+            self.add(at, SMALL, self.RS.at[2])
+
+        @pl.when((i == 2 + z) & (z < nz - 1))
+        def _():
+            up.start()
+
+        @pl.when((i == 3 + z) & (z < nz - 1))
+        def _():
+            up.wait_send()
+
+        @pl.when((i == nz + 1) & (z == nz - 1))
+        def _():
+            dst[...] = src[...]
+
+        @pl.when((i == 2 * nz - z) & (z < nz - 1))
+        def _():
+            down.wait_recv()
+
+        @pl.when((i == 2 * nz - z) & (z > 0))
+        def _():
+            down.start()
+
+        @pl.when((i == 2 * nz - z + 1) & (z > 0))
+        def _():
+            down.wait_send()
+
     def f_copy(self, c, k):
         a, dev = (self.x, self.px) if c == 0 else (self.y, self.py)
-        q = k % W
+        q = k % WF
         return self.copy(self.rows(self.base(c, k) + (1 - a) * (R // 2), R // 2), self.RF.at[c, q], "F", (c, q), dev)
 
     def first(self, c, i):
-        @pl.when(i < self.counts[c])
-        def _():
-            self.f_copy(c, i).start()
+        early = i < AHEAD
+        k = jnp.where(early, 2 * i, i + AHEAD)
+
+        @pl.when(k < self.counts[c])
+        def _():
+            self.f_copy(c, k).start()
+
+        @pl.when(early & (2 * i + 1 < self.counts[c]))
+        def _():
+            self.f_copy(c, 2 * i + 1).start()
 
     def rest(self, c, i):
         nz, z = self.nz, self.z
-        a, fdev, b, ldev = (self.x, self.px, self.y, self.py) if c == 0 else (self.y, self.py, self.x, self.px)
+        a, fdev, ldev = (self.x, self.px, self.py) if c == 0 else (self.y, self.py, self.px)
         n = self.counts[c]
-        H, Q, E = R // 2, R // 4, R // 8
+        H, Q = R // 2, R // 4
 
         def ok(k):
             return (k >= 0) & (k < n)
@@ -113,7 +187,7 @@
             cp = self.f_copy(c, k)
             cp.wait_send()
             cp.wait_recv()
-            self.add(half(k), H, self.RF.at[c, k % W])
+            self.add(half(k), H, self.RF.at[c, k % WF])
 
         def up(k, s):
             return self.copy(self.rows(sub(k, s), Q), self.RU.at[c, s, k % W], "U", (c, s, k % W), jnp.minimum(self.d + 4, 4 * nz - 1))
@@ -128,9 +202,13 @@
             def _(k=k, s=s):
                 up(k, s).wait_recv()
                 self.add(sub(k, s), Q, self.RU.at[c, s, k % W])
+                if self.credits:
+                    self.give(k + W < n, "CU", c, s, jnp.maximum(self.d - 4, 0))
 
             @pl.when(ok(k) & (z < root(k, s)))
             def _(k=k, s=s):
+                if self.credits:
+                    self.take(k >= W, "CU", c, s)
                 up(k, s).start()
 
             k = i - (LF + nz - 1 - z)
@@ -139,9 +217,13 @@
             def _(k=k, s=s):
                 dn(k, s).wait_recv()
                 self.add(sub(k, s), Q, self.RD.at[c, s, k % W])
+                if self.credits:
+                    self.give(k + W < n, "CD", c, s, jnp.minimum(self.d + 4, 4 * nz - 1))
 
             @pl.when(ok(k) & (z > root(k, s)))
             def _(k=k, s=s):
+                if self.credits:
+                    self.take(k >= W, "CD", c, s)
                 dn(k, s).start()
 
             k = i - (LF + z + 1)
@@ -156,30 +238,24 @@
             def _(k=k, s=s):
                 dn(k, s).wait_send()
 
-        def last(k, s):
-            return self.copy(self.rows(sub(k, s) + (1 - b) * E, E), self.RL.at[c, k % W], "L", (c, k % W), ldev)
-
-        def last_back(k, s):
-            at = sub(k, s) + b * E
-            return self.copy(self.rows(at, E), self.done(at, E), "M", (c, k % W), ldev)
+        def cross(k, s):
+            return self.copy(self.rows(sub(k, s), Q), self.RL.at[c, k % W], "L", (c, k % W), ldev)
 
         for s in (0, 1):
             k = i - (LF + nz - 1)
 
             @pl.when(ok(k) & (z == root(k, s)))
             def _(k=k, s=s):
-                last(k, s).start()
+                cross(k, s).start()
 
             k = i - (LF + nz)
 
             @pl.when(ok(k) & (z == root(k, s)))
             def _(k=k, s=s):
-                cp = last(k, s)
+                cp = cross(k, s)
                 cp.wait_send()
                 cp.wait_recv()
-                self.add(sub(k, s) + b * E, E, self.RL.at[c, k % W])
-                last_back(k, s).start()
-                self.done(sub(k, s) + b * E, E)[...] = self.rows(sub(k, s) + b * E, E)[...]
+                self.done(sub(k, s), Q)[...] = self.rows(sub(k, s), Q)[...] + self.RL[c, k % W]
 
         def g_up(k, s):
             r = self.done(sub(k, s), Q)
@@ -196,15 +272,9 @@
         for e in (0, 1):
             for s in (0, 1):
                 r = e if s == 0 else nz - 1 - e
-                lag = LF + nz + 1 + jnp.abs(z - r)
+                lag = LF + nz + jnp.abs(z - r)
                 k = i - lag
                 here = ok(k) & (k % 2 == e)
-
-                @pl.when(here & (z == r))
-                def _(k=k, s=s):
-                    cp = last_back(k, s)
-                    cp.wait_send()
-                    cp.wait_recv()
 
                 @pl.when(here & (z < r))
                 def _(k=k, s=s):
@@ -244,17 +314,19 @@
                     g_up(k, s).wait_send()
 
 
-KINDS = {"F": (2, W), "U": (2, 2, W), "D": (2, 2, W), "L": (2, W), "M": (2, W), "V": (2, 2, W), "E": (2, 2, W), "G": (2, 2, W)}
-SEMS = [k + e for k in KINDS for e in "sr"]
+KINDS = {"F": (2, WF), "U": (2, 2, W), "D": (2, 2, W), "L": (2, W), "V": (2, 2, W), "E": (2, 2, W), "G": (2, 2, W), "S": (4,)}
+SEMS = [k + e for k in KINDS for e in "sr" if k + e not in ("Ds", "Er")]
+CREDITS = ["CU", "CD"]
 
 
 def comm_scratch(width):
     return [
-        pltpu.VMEM((2, W, R // 2, width), jnp.float32),
+        pltpu.VMEM((2, WF, R // 2, width), jnp.float32),
         pltpu.VMEM((2, 2, W, R // 4, width), jnp.float32),
         pltpu.VMEM((2, 2, W, R // 4, width), jnp.float32),
-        pltpu.VMEM((2, W, R // 8, width), jnp.float32),
-    ] + [pltpu.SemaphoreType.DMA(KINDS[k[0]]) for k in SEMS]
+        pltpu.VMEM((2, W, R // 4, width), jnp.float32),
+        pltpu.VMEM((3, SMALL, width), jnp.float32),
+    ] + [pltpu.SemaphoreType.DMA(KINDS[k[0]]) for k in SEMS] + [pltpu.SemaphoreType.REGULAR((2, 2)) for _ in CREDITS]
 
 def f32dot(a, b, dims=((1,), (0,))):
     return lax.dot_general(a, b, (dims, ((), ())), preferred_element_type=jnp.float32)
@@ -308,12 +380,12 @@
 
 
 def layer_kernel(n, *refs):
-    (x_h, ids, ag_h, as_h, wp_h, pb_h, wo_h, ob_h, fg_h, fs_h, we_h, eb_h, ws_h, sb_h, go_h, cos_h, sin_h) = refs[:17]
+    (x_h, ids_h, ag_h, as_h, wp_h, pb_h, wo_h, ob_h, fg_h, fs_h, we_h, eb_h, ws_h, sb_h, go_h, cos_h, sin_h) = refs[:17]
     O, bo, gi = refs[17:20]
-    (x, ag, ash, wp, pb, wo, ob, fg, fs, we, eb, ws, sb, go, cos, sin) = refs[20:36]
+    (x, ids, ag, ash, wp, pb, wo, ob, fg, fs, we, eb, ws, sb, go, cos, sin) = refs[20:37]
     ag, ash, ob, fg, fs, eb, sb = (Row(v) for v in (ag, ash, ob, fg, fs, eb, sb))
-    (ain, qkv, att, prob, mid, ein, act, PX, RX, dqkv, G, RF, RU, RD, RL, local, xs, xr, ys, yr, bias2) = refs[36:57]
-    sems = dict(zip(SEMS, refs[57:]))
+    (ain, qkv, att, prob, mid, ein, act, PX, RX, dqkv, G, RF, RU, RD, RL, RS, local, xs, xr, ys, yr, bias2) = refs[37:59]
+    sems = dict(zip(SEMS + CREDITS, refs[59:]))
     T, D = x.shape
     WL = wo.shape[0]
     FL = ws.shape[0]
@@ -322,7 +394,7 @@
     base_out, base_pack = FL + D * (FL // D), FL + D * (FL // D) + WL
     base_small = base_pack + D + WL
     full = base_small // (2 * R)
-    comm = Comm(n, (full + 1, full), G, O, RF, RU, RD, RL, sems)
+    comm = Comm(n, (full, full), G, O, RF, RU, RD, RL, RS, sems)
     at_step = [0]
 
     def tick(more=0):
@@ -333,7 +405,7 @@
 
     loads = []
     for j, (src, dst) in enumerate(
-        [(x_h, x), (wp_h.at[0], wp.at[0]), (cos_h, cos), (sin_h, sin), (ag_h, ag.ref), (as_h, ash.ref), (pb_h, pb), (wo_h, wo), (ob_h, ob.ref), (fg_h, fg.ref), (fs_h, fs.ref), (we_h, we), (eb_h, eb.ref), (go_h, go), (ws_h, ws), (sb_h, sb.ref), (wp_h.at[1], wp.at[1]), (wp_h.at[2], wp.at[2])]
+        [(x_h, x), (wp_h.at[0], wp.at[0]), (cos_h, cos), (sin_h, sin), (ag_h, ag.ref), (as_h, ash.ref), (pb_h, pb), (wo_h, wo), (ob_h, ob.ref), (fg_h, fg.ref), (fs_h, fs.ref), (we_h, we), (eb_h, eb.ref), (go_h, go), (ws_h, ws), (sb_h, sb.ref), (wp_h.at[1], wp.at[1]), (wp_h.at[2], wp.at[2]), (ids_h, ids)]
     ):
         loads.append(pltpu.make_async_copy(src, dst, local.at[j]))
 
@@ -345,14 +417,14 @@
         for j in which:
             loads[j].wait()
 
-    begin(0, 4, 5, 1, 2, 3, 6, 16, 17)
+    begin(0, 4, 5, 18, 1, 2, 3, 6, 16, 17)
     comm.arrive()
-    arrived(0, 4, 5)
+    arrived(0, 4, 5, 18)
 
     lane = lax.broadcasted_iota(jnp.int32, (1, LANES), 1)
     low_half = (lane // (HEAD // 2)) % 2 == 0
     first_head = lane < HEAD
-    other = (ids[T - 1] > 0).astype(jnp.float32)
+    other = jnp.max(ids[...].reshape(1, T).astype(jnp.float32), axis=1, keepdims=True)
     col = lax.broadcasted_iota(jnp.int32, (1, T), 1)
     top_bias = jnp.where(col < half, 0.0, MASKED * other)
     low_bias = jnp.where(col < half, MASKED * other, 0.0)
@@ -400,7 +472,7 @@
     def swap(i, h):
         rows = pl.ds(pl.multiple_of(h * half, half), half)
         return pltpu.make_async_remote_copy(
-            src_ref=PX.at[i % 2, rows, :], dst_ref=RX.at[i % 2, rows, :], send_sem=xs.at[i, h], recv_sem=xr.at[i, h],
+            src_ref=PX.at[i % 2, rows, :], dst_ref=RX.at[i % 2, rows, :], send_sem=xs.at[i - 1, h], recv_sem=xr.at[i - 1, h],
             device_id=(comm.d, 1 - comm.t), device_id_type=MESH)
 
     arrived(7, 8, 9, 10)
@@ -409,17 +481,21 @@
     def attend(i, carry):
         rows = pl.ds(pl.multiple_of(i * QR, QR), QR)
         bias = jnp.where(i < blocks // 2, top_bias, low_bias)
+        scores, probs = [], []
         for j in range(parts):
-            keys, vals = qkv[parts + j], qkv[2 * parts + j]
             q = qkv[j, rows, :]
             zeros = jnp.zeros_like(q)
             two = jnp.concatenate([jnp.where(first_head, q, zeros), jnp.where(first_head, zeros, q)], axis=0)
-            s = f32dot(two, keys, NT) + bias
+            scores.append(f32dot(two, qkv[parts + j], NT) + bias)
+        for j in range(parts):
+            s = scores[j]
             p = jnp.exp(s - jnp.max(s, axis=-1, keepdims=True))
             p = (p * (1.0 / jnp.sum(p, axis=-1, keepdims=True))).astype(jnp.bfloat16)
             prob[2 * j, rows, :] = p[:QR]
             prob[2 * j + 1, rows, :] = p[QR:]
-            out = f32dot(p, vals)
+            probs.append(p)
+        for j in range(parts):
+            out = f32dot(probs[j], qkv[2 * parts + j])
             att[rows, j * LANES : (j + 1) * LANES] = jnp.where(first_head, out[:QR], out[QR:]).astype(jnp.bfloat16)
         PX[0, rows, :] = f32dot(att[rows, :], wo[...])
         first_swap(i).start()
@@ -652,10 +728,11 @@
     small_row(0)[...] = sums[0]
     small_row(1)[...] = sums[1]
     G[pl.ds(base_small + 8, 3), pl.ds(WL, D - WL)] = jnp.zeros((3, D - WL), jnp.float32)
-    G[pl.ds(base_small + 11, R - 11), :] = jnp.zeros((R - 11, D), jnp.float32)
+    G[pl.ds(base_small + 11, SMALL - 11), :] = jnp.zeros((SMALL - 11, D), jnp.float32)
 
     def body(i, carry):
         comm.step(i)
+        comm.small(i - at_step[0], base_small)
         return carry
 
     lax.fori_loop(at_step[0], comm.steps(), body, 0)
@@ -718,7 +795,7 @@
     parts = WL // LANES
     bf16, f32 = jnp.bfloat16, jnp.float32
     cosine, sine = tables(T)
-    total = FL + D * (FL // D) + WL + D + WL + R
+    total = FL + D * (FL // D) + WL + D + WL + SMALL
 
     args = [
         block_input,
@@ -741,12 +818,12 @@
     ]
     hbm = pl.BlockSpec(memory_space=pltpu.HBM)
     vmem = pl.BlockSpec(memory_space=pltpu.VMEM)
-    held = [pltpu.VMEM(a.shape, a.dtype) for i, a in enumerate(args) if i != 1]
+    held = [pltpu.VMEM(a.shape, a.dtype) for a in args]
     scratch = comm_scratch(D)
     whole, out, grad_in = pl.pallas_call(
         functools.partial(layer_kernel, n_dp),
         out_shape=[pltpu.VMEM((total, D), f32), pltpu.VMEM((T, D), bf16), pltpu.VMEM((T, D), bf16)],
-        in_specs=[hbm, pl.BlockSpec(memory_space=pltpu.SMEM)] + [hbm] * 15,
+        in_specs=[hbm] * 17,
         out_specs=[vmem] * 3,
         scratch_shapes=held
         + [
@@ -762,10 +839,10 @@
             pltpu.VMEM((3 * parts, T, LANES), bf16),
             pltpu.VMEM((total, D), f32),
         ]
-        + scratch[:4]
-        + [pltpu.SemaphoreType.DMA((18,)), pltpu.SemaphoreType.DMA((4, 2)), pltpu.SemaphoreType.DMA((4, 2))]
+        + scratch[:5]
+        + [pltpu.SemaphoreType.DMA((19,)), pltpu.SemaphoreType.DMA((3, 2)), pltpu.SemaphoreType.DMA((3, 2))]
         + [pltpu.SemaphoreType.DMA((T // 128,)), pltpu.SemaphoreType.DMA((T // 128,)), pltpu.VMEM((FL // WL, WL), f32)]
-        + scratch[4:],
+        + scratch[5:],
         compiler_params=pltpu.CompilerParams(
             collective_id=0, has_side_effects=True, vmem_limit_bytes=48 << 20
         ),

time: 231 us -> 221 us (0.957)
  Pallas kernels: 230 us -> 220 us
    pallas_call x1, Pallas kernels: 224 us -> 214 us  [body(): pl.pallas_call(functools.partial(layer_kernel, n_dp), out_shape=[pltpu.VM...]
where the time goes in v5:
time: 221 us
  Pallas kernels  220 us (100%)
    pallas_call x1, Pallas kernels, body(): pl.pallas_call(functools.partial(layer_kernel, n_dp), out_shape=[pltpu.VM...  214 us
    pallas_call x1, Pallas kernels, body(): pl.pallas_call(functools.partial(unpack, functools.partial(unpack_moves,...  6.46 us

profile of v5, /device:TPU:0, one launch (start us, length us, event | category | flops | bytes accessed | tf_op | source)
XLA Modules:
  0.0 221.1 jit_solution(7162127622307632818)
XLA Ops:
  0.7 213.8 %shard_map.272 = (f32[4624,768]{1,0:T(8,128)S(1)}, bf16[512,768]{1,0:T(8,128)(2,1)S(1)}, bf16[512,768]{1,0:T(8,128)(2,1)S(1)}) custom-call(bf16[512,768]{1,0:T(8,128)(2,1)} %refs_0_.1, s32[512]{0:T(512)} %refs_1_.1, f32[768]{0:T(1024)} %refs_2_.1, f32[768]{0:T(1024)} %refs_3_.1, bf16[3,768,384]{2,1,0:T(8,128)(2,1)} %bitcast.2, f32[3,384]{1,0:T(4,128)} %refs_5_.1, ...), custom_call_target="tpu_custom_call" | custom-call | tf_op jit(solution)/shard_map/pallas_call | solution.py:823
  214.5 6.5 %shard_map.273 = (bf16[512,768]{1,0:T(8,128)(2,1)}, bf16[512,768]{1,0:T(8,128)(2,1)}, f32[1536,768]{1,0:T(8,128)}, f32[768,1536]{1,0:T(8,128)}, f32[384,768]{1,0...) custom-call(f32[4624,768]{1,0:T(8,128)S(1)} %get-tuple-element.31.wh, ...), custom_call_target="tpu_custom_call" | custom-call | tf_op jit(solution)/shard_map/pallas_call | solution.py:862

commit v6 on v5

--- a/solution.py
+++ b/solution.py
@@ -437,7 +437,7 @@
         normed, _ = norm(x[rows, :].astype(jnp.float32))
         ain[rows, :] = (normed * ag[...] + ash[...]).astype(jnp.bfloat16)
 
-    chunks(T, 64, norm_in)
+    chunks(T, 64, norm_in, True)
     arrived(1, 2, 3, 6)
     begin(7, 8, 9, 10, 11, 12, 13, 14, 15)
     for table in (cos, sin):
@@ -458,9 +458,9 @@
                     v = v.astype(jnp.bfloat16) * jnp.bfloat16(HEAD**-0.5)
                 qkv[c * parts + j, rows, :] = v.astype(jnp.bfloat16)
 
-        chunks(T, 64, turn)
-
-    QR = 128
+        chunks(T, 64, turn, True)
+
+    QR = 256
     blocks = T // QR
 
     def first_swap(i):
@@ -541,7 +541,7 @@
             pre[rows, here] = v
             act[rows, cols] = (v * (0.5 + 0.5 * lax.erf(v * math.sqrt(0.5)))).astype(jnp.bfloat16)
 
-        chunks(T, 64, gelu_rows)
+        chunks(T, 64, gelu_rows, True)
         G[pl.ds(pl.multiple_of(b * NB, LANES), NB), :] = f32dot(act[:, cols], go[...], TN)
         tick(b)
         return carry
@@ -653,8 +653,8 @@
         at = pl.ds(pl.multiple_of(j * LANES, LANES), LANES)
         dv = [None, None]
         dk = [None, None]
-        for r in range(0, T, QR):
-            rows = pl.ds(r, QR)
+        for r in range(0, T, 128):
+            rows = pl.ds(r, 128)
             do = att[rows, at]
             q = qkv[j, rows, :]
             dq = []
@@ -672,8 +672,8 @@
                 dk[e] = add_k if r == 0 else dk[e] + add_k
             v = jnp.where(first_head, *dq) * (HEAD**-0.5)
             dqkv[j, rows, :] = (v * cos[rows, :] - swap_halves(v, low_half) * sin[rows, :]).astype(jnp.bfloat16)
-            if (r // QR) % 2 == 1:
-                tick(2 * j + r // (2 * QR))
+            if (r // 128) % 2 == 1:
+                tick(2 * j + r // (2 * 128))
         dqkv[2 * parts + j] = jnp.where(first_head, *dv).astype(jnp.bfloat16)
         v = jnp.where(first_head, *dk)
         dqkv[parts + j] = (v * cos[...] - swap_halves(v, low_half) * sin[...]).astype(jnp.bfloat16)

time: 221 us -> 217 us (0.982)
  Pallas kernels: 220 us -> 216 us
    pallas_call x1, Pallas kernels: 214 us -> 210 us  [body(): pl.pallas_call(functools.partial(layer_kernel, n_dp), out_shape=[pltpu.VM...]
where the time goes in v6:
time: 217 us
  Pallas kernels  216 us (100%)
    pallas_call x1, Pallas kernels, body(): pl.pallas_call(functools.partial(layer_kernel, n_dp), out_shape=[pltpu.VM...  210 us
    pallas_call x1, Pallas kernels, body(): pl.pallas_call(functools.partial(unpack, functools.partial(unpack_moves,...  6.46 us

profile of v6, /device:TPU:0, one launch (start us, length us, event | category | flops | bytes accessed | tf_op | source)
XLA Modules:
  0.0 217.3 jit_solution(10348947933509300862)
XLA Ops:
  0.7 210.0 %shard_map.272 = (f32[4624,768]{1,0:T(8,128)S(1)}, bf16[512,768]{1,0:T(8,128)(2,1)S(1)}, bf16[512,768]{1,0:T(8,128)(2,1)S(1)}) custom-call(bf16[512,768]{1,0:T(8,128)(2,1)} %refs_0_.1, s32[512]{0:T(512)} %refs_1_.1, f32[768]{0:T(1024)} %refs_2_.1, f32[768]{0:T(1024)} %refs_3_.1, bf16[3,768,384]{2,1,0:T(8,128)(2,1)} %bitcast.2, f32[3,384]{1,0:T(4,128)} %refs_5_.1, ...), custom_call_target="tpu_custom_call" | custom-call | tf_op jit(solution)/shard_map/pallas_call | solution.py:823
  210.7 6.5 %shard_map.273 = (bf16[512,768]{1,0:T(8,128)(2,1)}, bf16[512,768]{1,0:T(8,128)(2,1)}, f32[1536,768]{1,0:T(8,128)}, f32[768,1536]{1,0:T(8,128)}, f32[384,768]{1,0...) custom-call(f32[4624,768]{1,0:T(8,128)S(1)} %get-tuple-element.31.wh, ...), custom_call_target="tpu_custom_call" | custom-call | tf_op jit(solution)/shard_map/pallas_call | solution.py:862
